TPU v7x, 32 devices: a whole 2x2x4 slice. The times are simulated.
32 devices in a mesh: member: 4 (over z), space: 8 (over y, x, core).
Axes of the slice: x: 2, y: 2, z: 4, core: 2. Of those that a mesh axis runs over, the one named last changes fastest.
Arguments:
- latent_state: bfloat16 [32, 128, 640], P('space'), may hold values from -6 to 6
- member_noise: bfloat16 [8, 32, 128, 640], P('member', 'space'), may hold values from -6 to 6
- conv_weight: float32 [9, 640], replicated, may hold values from -2 to 2
- norm_gain: float32 [640], replicated, may hold values from 0.1 to 1.9
- weight_in: bfloat16 [1920, 640], replicated, may hold values from -0.25 to 0.25
- weight_down: bfloat16 [1920, 640], replicated, may hold values from -0.125 to 0.125
- weight_head: bfloat16 [640, 320], replicated, may hold values from -0.25 to 0.25
- target_field: float32 [32, 128, 320], P('space'), may hold values from -6 to 6
Outputs:
- grad_in: float32 [1920, 640], P(('member', 'space'))
- grad_down: float32 [1920, 640], P(('member', 'space'))
- grad_head: float32 [640, 320], replicated
- grad_gain: float32 [640], replicated
- grad_conv: float32 [9, 640], replicated
All inputs are finite; a program needn't handle non-finite values.
Results may differ from a plain program's by a relative error of at most 0.007.
Values may be sent and summed in bfloat16 or wider, within the bound.
No kernel may reach another device: no remote copies, remote signals or barrier semaphores. Data moves between devices by JAX's collectives and lax.ppermute only.
A program may use at most 128 MiB of HBM per device.

v0:
```python
import functools
import math

import jax
import jax.numpy as jnp
from jax import lax
from jax.experimental import pallas as pl
from jax.experimental.pallas import tpu as pltpu
from jax.sharding import PartitionSpec as P


F32 = jnp.float32
SMALL = 10
BF16 = jnp.bfloat16
LAST = (((1,), (1,)), ((), ()))
FIRST = (((0,), (0,)), ((), ()))
SMEM = pl.BlockSpec(memory_space=pltpu.SMEM)


def dot(left, right, dims=(((1,), (0,)), ((), ()))):
    return lax.dot_general(left, right, dims, preferred_element_type=F32)


def ring(count, step):
    return [(i, (i + step) % count) for i in range(count)]


def flip(count, bit):
    return [(i, i ^ bit) for i in range(count)]


def size_of(shape, kind):
    return math.prod(shape) * jnp.dtype(kind).itemsize


def call(kernel, ins, outs, scratch, micros, scalars=1, room=6):
    kept = sum(size_of(part.shape, part.dtype) for part in scratch)
    moved = sum(size_of(x.shape, x.dtype) for x in ins) + sum(size_of(*out) for out in outs)
    return pl.pallas_call(
        kernel,
        in_specs=[SMEM] * scalars
        + [pl.BlockSpec(memory_space=pltpu.VMEM)] * (len(ins) - scalars),
        out_specs=[pl.BlockSpec(memory_space=pltpu.VMEM)] * len(outs),
        out_shape=[jax.ShapeDtypeStruct(shape, kind) for shape, kind in outs],
        scratch_shapes=scratch,
        compiler_params=pltpu.CompilerParams(vmem_limit_bytes=kept + (room << 20)),
        cost_estimate=pl.CostEstimate(
            flops=int(micros * 1e9), bytes_accessed=moved, transcendentals=0
        ),
    )(*ins)


def tile_of(total):
    return next(t for t in range(640, 0, -128) if total % t == 0)


def mixed_row(mixed, edges, m, i):
    if i < 0:
        return edges[0][m, 0]
    if i >= mixed.shape[1]:
        return edges[1][m, 0]
    return mixed[m, i]


def forward_kernel(rows, members, members_all, edged, *refs):
    me_ref, mixed = refs[:2]
    edges = refs[2:4] if edged else ()
    conv_w, gain, w_in, w_down, w_head, target = refs[2 + len(edges) : 8 + len(edges)]
    rest = refs[8 + len(edges) :]
    normed, normal, inv, activ, slope, hidden, attract = rest[:7]
    sends = rest[7 : 7 + members]
    mix_s, pred = rest[7 + members :]
    mem_dev, _, lon, _ = mixed.shape
    span = len(rows) * lon
    tile = tile_of(w_in.shape[0])
    me = me_ref[0]

    def conv_step(m, carry):
        for at, i in enumerate(rows):
            start = pl.multiple_of(m * span + at * lon, lon)
            here = pl.ds(start, lon)
            sums = [None] * 3
            for a in range(3):
                row_b = mixed_row(mixed, edges, m, i + a - 1)
                if a == 1:
                    mix_s[here, :] = row_b
                row = row_b.astype(F32)
                for b in range(3):
                    k = 3 * a + b
                    term = conv_w[k : k + 1, :] * row
                    sums[b] = term if sums[b] is None else sums[b] + term
            conv = (
                sums[1] + pltpu.roll(sums[0], 1, axis=0) + pltpu.roll(sums[2], lon - 1, axis=0)
            )
            center = conv - jnp.mean(conv, axis=-1, keepdims=True)
            scale = lax.rsqrt(jnp.mean(center * center, axis=-1, keepdims=True) + 1e-05)
            unit = center * scale
            normal[here, :] = unit
            inv[here, :] = jnp.broadcast_to(scale, (lon, 128))
            normed[here, :] = (unit * gain[...]).astype(BF16)
        return carry

    lax.fori_loop(0, mem_dev, conv_step, 0)
    rate = math.sqrt(2.0 / math.pi)
    for t in range(w_in.shape[0] // tile):
        at = pl.ds(t * tile, tile)
        x = dot(normed[...], w_in[at, :], LAST)
        linear = rate * x
        bend = 1.0 + 0.044715 * (x * x)
        tanh = jnp.tanh(linear * bend)
        half = 0.5 + 0.5 * tanh
        activ[:, at] = (x * half).astype(BF16)
        slope[:, at] = (
            half * (1.0 + (1.0 - tanh) * (linear * (3.0 * bend - 2.0)))
        ).astype(BF16)
    hid = (mix_s[...].astype(F32) + dot(activ[...], w_down[...])).astype(BF16)
    hidden[...] = hid
    pred[...] = dot(hid, w_head[...], LAST)
    for m in range(mem_dev):
        for at, i in enumerate(rows):
            here = pl.ds(m * span + at * lon, lon)
            error = pred[here, :] - target[i].T
            dist = lax.rsqrt(jnp.sum(error * error, axis=-1, keepdims=True) + 1.0)
            attract[here, :] = error * dist * (1.0 / members_all)
    points = span // members
    for k in range(members):
        chunk = lax.rem(me + k, members)
        for m in range(mem_dev):
            at = pl.ds(pl.multiple_of(m * span + chunk * points, points), points)
            sends[k][m] = pred[at, :].astype(BF16)


def forward(me, mixed, edges, conv_w, gain, w_in, w_down, w_head, target, rows, members):
    mem_dev, _, lon, width = mixed.shape
    out_width = w_head.shape[0]
    units = w_in.shape[0]
    total = mem_dev * len(rows) * lon
    points = len(rows) * lon // members
    ins = [me, mixed, *edges, conv_w, gain, w_in, w_down, w_head, target]
    outs = [
        ((total, width), BF16),
        ((total, width), F32),
        ((total, 128), F32),
        ((total, units), BF16),
        ((total, units), BF16),
        ((total, width), BF16),
        ((total, out_width), F32),
    ] + [((mem_dev, points, out_width), BF16)] * members
    scratch = [
        pltpu.VMEM((total, width), BF16),
        pltpu.VMEM((total, out_width), F32),
    ]
    kernel = functools.partial(
        forward_kernel, rows, members, members * mem_dev, len(edges) > 0
    )
    out = call(kernel, ins, outs, scratch, 9)
    return out[:7], out[7:]


def pair_kernel(*refs):
    half = len(refs) // 2
    ins, outs = refs[:half], refs[half:]
    per, points = ins[0].shape[:2]
    step = 16 if points % 16 == 0 else points

    def run(t, carry):
        at = pl.ds(pl.multiple_of(t * step, step), step)
        values = [ref[m, at, :].astype(F32) for ref in ins for m in range(per)]
        pulls = [None] * len(values)
        for a in range(len(values)):
            for b in range(a + 1, len(values)):
                gap = values[a] - values[b]
                pull = gap * lax.rsqrt(jnp.sum(gap * gap, axis=-1, keepdims=True) + 1.0)
                pulls[a] = pull if pulls[a] is None else pulls[a] + pull
                pulls[b] = -pull if pulls[b] is None else pulls[b] - pull
        for index, pull in enumerate(pulls):
            outs[index // per][index % per, at, :] = pull.astype(BF16)
        return carry

    lax.fori_loop(0, points // step, run, 0)


def pair_pull(groups):
    return call(pair_kernel, groups, [(groups[0].shape, BF16)] * len(groups), [], 2, 0)


def slope_kernel(members, scale, share, *refs):
    me_ref, attract = refs[:2]
    pulls = refs[2 : 2 + members]
    w_head, w_down, slope, grad, ghid, gpre = refs[2 + members :]
    mem_dev, points, _ = pulls[0].shape
    span = attract.shape[0] // mem_dev
    tile = tile_of(w_down.shape[0])
    me = me_ref[0]
    for k in range(members):
        chunk = lax.rem(me + k, members)
        for m in range(mem_dev):
            at = pl.ds(pl.multiple_of(m * span + chunk * points, points), points)
            grad[at, :] = (scale * (attract[at, :] - pulls[k][m].astype(F32) * share)).astype(BF16)
    ghid[...] = dot(grad[...], w_head[...]).astype(BF16)

    def unit_step(t, carry):
        at = pl.ds(pl.multiple_of(t * tile, tile), tile)
        back = dot(ghid[...], w_down[at, :], LAST)
        gpre[:, at] = (slope[:, at].astype(F32) * back).astype(BF16)
        return carry

    lax.fori_loop(0, w_down.shape[0] // tile, unit_step, 0)


def slopes(me, attract, pulls, w_head, w_down, slope, scale, share):
    total, out_width = attract.shape
    outs = [
        ((total, out_width), BF16),
        ((total, w_head.shape[1]), BF16),
        (slope.shape, BF16),
    ]
    kernel = functools.partial(slope_kernel, len(pulls), scale, share)
    ins = [me, attract, *pulls, w_head, w_down, slope]
    return call(kernel, ins, outs, [], 3)


def norm_kernel(rows, edged, *refs):
    gpre, w_in, normal, inv, gain, mixed = refs[:6]
    edges = refs[6:8] if edged else ()
    small, acc = refs[6 + len(edges) :]
    mem_dev, _, lon, _ = mixed.shape
    span = len(rows) * lon
    acc[...] = dot(gpre[...], w_in[...])
    small[...] = jnp.zeros(small.shape, F32)

    def conv_step(m, carry):
        for at, i in enumerate(rows):
            here = pl.ds(pl.multiple_of(m * span + at * lon, lon), lon)
            back = acc[here, :]
            unit = normal[here, :]
            product = back * unit
            small[9:10, :] += jnp.sum(product, axis=0, keepdims=True)
            g = back * gain[...]
            mean = jnp.mean(g, axis=-1, keepdims=True)
            along = jnp.mean(product * gain[...], axis=-1, keepdims=True)
            out = (g - mean - unit * along) * inv[here, 0:1]
            turned = [pltpu.roll(out, lon - 1, axis=0), out, pltpu.roll(out, 1, axis=0)]
            for a in range(3):
                row = mixed_row(mixed, edges, m, i + a - 1).astype(F32)
                for b in range(3):
                    k = 3 * a + b
                    small[k : k + 1, :] += jnp.sum(row * turned[b], axis=0, keepdims=True)
        return carry

    lax.fori_loop(0, mem_dev, conv_step, 0)


def norms(gpre, w_in, normal, inv, gain, mixed, edges, rows):
    width = w_in.shape[1]
    ins = [gpre, w_in, normal, inv, gain, mixed, *edges]
    kernel = functools.partial(norm_kernel, rows, len(edges) > 0)
    scratch = [pltpu.VMEM(normal.shape, F32)]
    return call(kernel, ins, [((16, width), F32)], scratch, 5, 0)[0]


def emit(source, low, keep, send, j, per):
    rows = keep.shape[1]
    even = source[2 * j * per : 2 * j * per + rows, :]
    odd = source[(2 * j + 1) * per : (2 * j + 1) * per + rows, :]
    keep[j] = jnp.where(low, even, odd)
    send[j] = jnp.where(low, odd, even).astype(BF16)


def weight_kernel(units, info_ref, left_a, left_b, right_a, right_b, keep, send, acc):
    size = left_a.shape[1]
    tile = tile_of(size)
    low = info_ref[1] == 0
    acc[size:, :] = jnp.zeros((acc.shape[0] - size, acc.shape[1]), F32)
    done = 0
    for t in range(size // tile):
        at = pl.ds(t * tile, tile)
        acc[at, :] = dot(left_a[:, at], right_a[...], FIRST) + dot(
            left_b[:, at], right_b[...], FIRST
        )
        while done < keep.shape[0] and (
            t == size // tile - 1 or (2 * done + 1) * units + keep.shape[1] <= (t + 1) * tile
        ):
            emit(acc, low, keep, send, done, units)
            done += 1


def pad_to(value, unit):
    return -(-value // unit) * unit


def weights(info, left, right, devices):
    size = left[0].shape[1]
    width = right[0].shape[1]
    units = size // devices
    rows = pad_to(units, 16)
    scratch = [pltpu.VMEM((pad_to(size + rows - units, 8) + 8, width), F32)]
    outs = [((devices // 2, rows, width), F32), ((devices // 2, rows, width), BF16)]
    kernel = functools.partial(weight_kernel, units)
    return call(kernel, [info, *left, *right], outs, scratch, 6)


def head_kernel(head_rows, info_ref, *refs):
    grads, hids, smalls = refs[0:2], refs[2:4], refs[4:6]
    keep, send, plain, head = refs[6:]
    wide = grads[0].shape[1]
    plain[0:wide, :] = dot(grads[0][...], hids[0][...], FIRST) + dot(
        grads[1][...], hids[1][...], FIRST
    )
    small = smalls[0][...] + smalls[1][...]
    head[...] = jnp.zeros(head.shape, F32)
    slot = keep.shape[1]
    for block in range(head.shape[0] // slot):
        rows = min(head_rows, max(0, wide - block * head_rows))
        if rows:
            head[block * slot : block * slot + rows, :] = plain[
                block * head_rows : block * head_rows + rows, :
            ]
        if block < SMALL:
            at = block * slot + head_rows
            head[at : at + 1, :] = small[block : block + 1, :]
    low = info_ref[1] == 0
    for j in range(keep.shape[0]):
        emit(head, low, keep, send, j, slot)


def heads(info, grads, hids, smalls, devices):
    wide = grads[0].shape[1]
    width = hids[0].shape[1]
    head_rows = -(-wide // devices)
    slot = pad_to(head_rows + 1, 16)
    scratch = [pltpu.VMEM((wide, width), F32), pltpu.VMEM((devices * slot, width), F32)]
    outs = [((devices // 2, slot, width), F32), ((devices // 2, slot, width), BF16)]
    kernel = functools.partial(head_kernel, head_rows)
    return call(kernel, [info, *grads, *hids, *smalls], outs, scratch, 2)


def insert(index, place, bit):
    low = (1 << place) - 1
    return ((index >> place) << (place + 1)) | (bit << place) | (index & low)


def merge_kernel(plans, shared, info_ref, *refs):
    count = len(plans)
    given = 1 if shared else count
    keeps, gots = refs[:given], refs[given : 2 * given]
    outs = refs[2 * given :]
    if shared:
        keeps, gots = keeps * count, gots * count
    for flow, (first, rows, place, which) in enumerate(plans):
        bit = info_ref[1 + which]
        keep, got = keeps[flow], gots[flow]
        out_keep, out_send = outs[2 * flow : 2 * flow + 2]
        at = pl.ds(first, rows)

        def step(i, carry, keep=keep, got=got, out_keep=out_keep, out_send=out_send, at=at, place=place, bit=bit):
            mine = insert(i, place, bit)
            other = insert(i, place, 1 - bit)
            out_keep[i] = keep[mine, at, :] + got[mine, at, :].astype(F32)
            out_send[i] = (keep[other, at, :] + got[other, at, :].astype(F32)).astype(BF16)
            return carry

        lax.fori_loop(0, out_keep.shape[0], step, 0)


def merge(info, keeps, gots, plans):
    width = keeps[0].shape[2]
    outs = []
    for keep, (_, rows, _, _) in zip(keeps, plans):
        blocks = keep.shape[0] // 2
        outs += [((blocks, rows, width), F32), ((blocks, rows, width), BF16)]
    shared = keeps[0] is keeps[-1]
    kernel = functools.partial(merge_kernel, plans, shared)
    if shared:
        keeps, gots = keeps[:1], gots[:1]
    out = call(kernel, [info, *keeps, *gots], outs, [], 1)
    return out[0::2], out[1::2]


def turn_kernel(members, firsts, info_ref, *refs):
    count = len(firsts)
    keeps, gots = refs[:count], refs[count : 2 * count]
    outs = refs[2 * count :]
    for k in range(members):
        block = lax.rem(info_ref[0] + k, members)
        for flow, first in enumerate(firsts):
            value = keeps[flow][block] + gots[flow][block].astype(F32)
            outs[k][first : first + value.shape[0], :] = value.astype(outs[k].dtype)


def turn(info, keeps, gots, members):
    width = keeps[0].shape[2]
    firsts, rows = [], 0
    for keep in keeps:
        firsts.append(rows)
        rows += keep.shape[1]
    outs = [((rows, width), F32)] + [((rows, width), BF16)] * (members - 1)
    kernel = functools.partial(turn_kernel, members, tuple(firsts))
    return call(kernel, [info, *keeps, *gots], outs, [], 1)


def start_blocks(send):
    return lax.ppermute(send, "space", flip(lax.axis_size("space"), 1))


def flows_of(rows):
    levels = list(range(1, lax.axis_size("space").bit_length() - 1))
    cut = pad_to(rows, 32) // 2
    flows = [(0, cut, levels)]
    if rows > cut:
        flows.append((cut, rows - cut, levels[::-1]))
    return flows


def merge_blocks(info, keeps, gots, flows, depth):
    spaces = lax.axis_size("space")
    plans = []
    for first, size, order in flows:
        place = sum(1 for other in order[depth:] if other < order[depth])
        plans.append((first if depth == 0 else 0, size, place, order[depth]))
    keeps, sends = merge(info, keeps, gots, tuple(plans))
    gots = [
        lax.ppermute(part, "space", flip(spaces, 1 << order[depth]))
        for part, (_, _, order) in zip(sends, flows)
    ]
    return list(keeps), list(gots)


def turn_blocks(info, keeps, gots):
    members = lax.axis_size("member")
    parts = turn(info, keeps, gots, members)
    return parts[0], [
        lax.ppermute(parts[k], "member", ring(members, k)) for k in range(1, members)
    ]


def add_up(own, others):
    for other in others:
        own = own + other.astype(F32)
    return own


def round_kernel(info_ref, keep, got, own):
    own[...] = (keep[...] + got[...].astype(F32)).astype(BF16)


def fold_kernel(info_ref, *refs):
    pieces, out, hold = refs[:-2], refs[-2], refs[-1]
    members = len(pieces)
    for k in range(members):
        hold[k] = pieces[k][...].astype(F32)
    total = hold[info_ref[0]]
    for m in range(1, members):
        total = total + hold[lax.rem(info_ref[0] + members - m, members)]
    out[...] = total.astype(BF16)


def turned(index, count):
    bits = count.bit_length() - 1
    return sum(((index >> b) & 1) << (bits - 1 - b) for b in range(bits))


def place_kernel(info_ref, rel, out):
    spaces, members = rel.shape[:2]
    place = 0
    for bit in range(spaces.bit_length() - 1):
        place = place + info_ref[1 + bit] * (1 << bit)
    for r in range(spaces):
        for m in range(members):
            out[m * spaces + (place ^ turned(r, spaces))] = rel[r, m].astype(F32)


def fold_members(info, keep, got):
    members = lax.axis_size("member")
    own = call(round_kernel, [info, keep, got], [(keep.shape, BF16)], [], 1)[0]
    return own, [lax.ppermute(own, "member", ring(members, k)) for k in range(1, members)]


def fold(info, pieces):
    scratch = [pltpu.VMEM((len(pieces),) + pieces[0].shape, F32)]
    return call(fold_kernel, [info, *pieces], [(pieces[0].shape, BF16)], scratch, 1)[0]


def spread_step(whole, bit):
    other = lax.ppermute(whole, "space", flip(lax.axis_size("space"), bit))
    return jnp.concatenate([whole, other], axis=0)


def placed(info, whole):
    spaces, members = whole.shape[:2]
    outs = [((members * spaces,) + whole.shape[2:], F32)]
    return call(place_kernel, [info, whole], outs, [], 1)[0]


def after(value, other):
    return lax.optimization_barrier((value, other))


def mix_kernel(info_ref, latent, noise, mixed, first, last):
    mem_dev, lat = noise.shape[:2]
    for i in range(lat):
        for m in range(mem_dev):
            value = (latent[i].astype(F32) + noise[m, i].astype(F32)).astype(BF16)
            mixed[m, i] = value
            if i == 0:
                first[m, 0] = value
            if i == lat - 1:
                last[m, 0] = value


def mix_rows(info, latent, noise):
    mem_dev, _, lon, width = noise.shape
    edge = ((mem_dev, 1, lon, width), BF16)
    outs = [(noise.shape, BF16), edge, edge]
    return call(mix_kernel, [info, latent, noise], outs, [], 1)


def body(
    latent_state,
    member_noise,
    conv_weight,
    norm_gain,
    weight_in,
    weight_down,
    weight_head,
    target_field,
):
    mem_dev, lat_dev, lon_len, width = member_noise.shape
    out_width = weight_head.shape[1]
    members = lax.axis_size("member")
    spaces = lax.axis_size("space")
    devices = members * spaces
    members_all = mem_dev * members
    points_all = lat_dev * spaces * lon_len
    scale = math.sqrt(members_all * out_width / points_all)
    share = 1.0 / (members_all * (members_all - 1))
    place = lax.axis_index("space")
    info = jnp.stack(
        [lax.axis_index("member")] + [(place >> b) & 1 for b in range(spaces.bit_length() - 1)]
    ).astype(jnp.int32)
    gain = norm_gain.reshape(1, width)
    head_t = weight_head.T
    target_t = target_field.transpose(0, 2, 1)

    mixed, first, last = mix_rows(info, latent_state, member_noise)
    above = lax.ppermute(last, "space", [(i, i + 1) for i in range(spaces - 1)])
    below = lax.ppermute(first, "space", [(i + 1, i) for i in range(spaces - 1)])
    halves = [(tuple(range(1, lat_dev - 1)), ()), ((0, lat_dev - 1), (above, below))]

    saved, pulled = [], []
    for rows, edges in halves:
        kept, sends = forward(
            info, mixed, edges, conv_weight, gain,
            weight_in, weight_down, head_t, target_t, rows, members,
        )
        saved.append(kept)
        pulled.append(
            [sends[0]]
            + [lax.ppermute(sends[k], "member", ring(members, k)) for k in range(1, members)]
        )
    pulled[0][-1], pulled[1][0] = lax.optimization_barrier((pulled[0][-1], pulled[1][0]))
    backs = []
    for half in range(2):
        pulls = pair_pull(pulled[half])
        backs.append(
            [pulls[0]]
            + [
                lax.ppermute(pulls[k], "member", ring(members, members - k))
                for k in range(1, members)
            ]
        )
    backs[0][0], backs[1][0] = lax.optimization_barrier((backs[0][0], backs[1][0]))
    grads, smalls = [], []
    for half, (rows, edges) in enumerate(halves):
        _, normal, inv, _, slope, _, attract = saved[half]
        if half:
            attract, smalls[0] = lax.optimization_barrier((attract, smalls[0]))
        grads.append(
            slopes(info, attract, backs[half], head_t, weight_down, slope, scale, share)
        )
        smalls.append(
            norms(
                grads[half][2], weight_in, normal, inv, gain, mixed, edges, rows,
            )
        )

    hids = [saved[h][5] for h in range(2)]
    keep_h, send_h = heads(info, [grads[h][0] for h in range(2)], hids, smalls, devices)
    got_h = start_blocks(send_h)
    keep_d, send_d = weights(
        info, [saved[h][3] for h in range(2)], [grads[h][1] for h in range(2)], devices
    )
    got_d = start_blocks(send_d)
    flows_h, flows_d = flows_of(keep_h.shape[1]), flows_of(keep_d.shape[1])
    keep_h, keep_d = after(keep_h, keep_d)
    part_h = merge_blocks(info, [keep_h], [got_h], flows_h, 0)
    gpre = [grads[h][2] for h in range(2)]
    gpre[1], part_h[0][0] = after(gpre[1], part_h[0][0])
    keep_i, send_i = weights(info, gpre, [saved[h][0] for h in range(2)], devices)
    got_i = start_blocks(send_i)
    part_h[0][0], keep_i = after(part_h[0][0], keep_i)
    depths = spaces.bit_length() - 2
    for depth in range(1, depths):
        part_h = merge_blocks(info, *part_h, flows_h, depth)
    keep_d, part_h[0][0] = after(keep_d, part_h[0][0])
    part_d = [keep_d] * len(flows_d), [got_d] * len(flows_d)
    part_d = merge_blocks(info, *part_d, flows_d, 0)
    keep_i, part_d[0][0] = after(keep_i, part_d[0][0])
    part_i = [keep_i] * len(flows_d), [got_i] * len(flows_d)
    part_i = merge_blocks(info, *part_i, flows_d, 0)
    part_h[0][0], part_i[0][0] = after(part_h[0][0], part_i[0][0])
    own_h, others_h = fold_members(info, part_h[0][0], part_h[1][0])
    part_d[0][0], own_h = after(part_d[0][0], own_h)
    for depth in range(1, depths):
        part_d = merge_blocks(info, *part_d, flows_d, depth)
        part_i[0][0], part_d[0][0] = after(part_i[0][0], part_d[0][0])
        part_i = merge_blocks(info, *part_i, flows_d, depth)
        part_d[0][0], part_i[0][0] = after(part_d[0][0], part_i[0][0])
    own_h, part_i[0][0] = after(own_h, part_i[0][0])
    whole = fold(info, [own_h, *others_h])[None]
    bit = spaces // 2
    whole = spread_step(whole, bit)
    own_d, others_d = turn_blocks(info, *part_d)
    part_i[0][0], own_d = after(part_i[0][0], own_d)
    own_i, others_i = turn_blocks(info, *part_i)
    whole, own_i = after(whole, own_i)
    while bit > 1:
        bit //= 2
        whole = spread_step(whole, bit)
    gathered = placed(info, whole)
    units = weight_in.shape[0] // devices
    head_rows = -(-out_width // devices)
    head_total = gathered[:, :head_rows].reshape(-1, width)[:out_width].T
    small = gathered[:SMALL, head_rows]
    in_mine = add_up(own_i, others_i)[:units]
    down_mine = add_up(own_d, others_d)[:units]
    return (in_mine, down_mine, head_total, small[9], small[:9])


def solution(mesh):
    return jax.shard_map(
        body,
        mesh=mesh,
        in_specs=(
            P("space", None, None),
            P("member", "space", None, None),
            P(),
            P(),
            P(),
            P(),
            P(),
            P("space", None, None),
        ),
        out_specs=(P(("member", "space"), None), P(("member", "space"), None), P(), P(), P()),
        check_vma=False,
    )
```

profile of v0, /device:TPU:0, one launch (start us, length us, event | category | flops | bytes accessed | tf_op | source)
XLA Modules:
  0.0 147.8 jit_solution(14286347220976247809)
XLA Ops:
  4.2 2.4 %collective-permute-start = (bf16[2,1,128,640]{3,2,1,0:T(8,128)(2,1)S(1)}, bf16[2,1,128,640]{3,2,1,0:T(8,128)(2,1)S(1)}, u32[]{:S(2)}, u32[]{:S(2)}) collective-permute-start(bf16[2,1,128,640]{3,2,1,0:T(8,128)(2,1)S(1)} %get-tuple-element.109), channel_id=1, source_target_pairs={{0,1},{1,2},{2,3},{3,4},{4,5},{5,6},{6,7},{8,9},{9,10},{10,11},{11... | collective-permute-start | bytes 983048 | tf_op jit(solution)/shard_map/ppermute | solution.py:546
  9.6 7.7 %shard_map.121 = (bf16[512,640]{1,0:T(8,128)(2,1)S(1)}, f32[512,640]{1,0:T(8,128)S(1)}, f32[512,128]{1,0:T(8,128)S(1)}, bf16[512,1920]{1,0:T(8,128)(2,1)S(1)}, b...) custom-call(s32[4]{0:T(128)S(1)} %pad_add_fusion.info_ref.refs_0_, ...), custom_call_target="tpu_custom_call" | custom-call | flops 8999999488 | bytes 15115280 | tf_op jit(solution)/shard_map/pallas_call | solution.py:39
  17.3 2.4 %collective-permute-start.2 = (bf16[2,64,320]{2,1,0:T(8,128)(2,1)S(1)}, bf16[2,64,320]{2,1,0:T(8,128)(2,1)S(1)}, u32[]{:S(2)}, u32[]{:S(2)}) collective-permute-start(bf16[2,64,320]{2,1,0:T(8,128)(2,1)S(1)} %get-tuple-element.114), channel_id=1, source_target_pairs={{0,8},{8,16},{16,24},{24,0},{1,9},{9,17},{17,25},{25,1},{2,10},{10... | collective-permute-start | bytes 245768 | tf_op jit(solution)/shard_map/ppermute | solution.py:559
  19.8 2.6 %collective-permute-start.3 = (bf16[2,64,320]{2,1,0:T(8,128)(2,1)S(1)}, bf16[2,64,320]{2,1,0:T(8,128)(2,1)S(1)}, u32[]{:S(2)}, u32[]{:S(2)}) collective-permute-start(bf16[2,64,320]{2,1,0:T(8,128)(2,1)S(1)} %get-tuple-element.115), channel_id=1, source_target_pairs={{0,16},{8,24},{16,0},{24,8},{1,17},{9,25},{17,1},{25,9},{2,18},{10... | collective-permute-start | bytes 245768 | tf_op jit(solution)/shard_map/ppermute | solution.py:559
  23.7 7.7 %shard_map.120 = (bf16[512,640]{1,0:T(8,128)(2,1)S(1)}, f32[512,640]{1,0:T(8,128)S(1)}, f32[512,128]{1,0:T(8,128)S(1)}, bf16[512,1920]{1,0:T(8,128)(2,1)S(1)}, b...) custom-call(s32[4]{0:T(128)S(1)} %pad_add_fusion.info_ref.refs_0_, ...), custom_call_target="tpu_custom_call" | custom-call | flops 8999999488 | bytes 15770640 | tf_op jit(solution)/shard_map/pallas_call | solution.py:39
  32.6 2.8 %collective-permute-start.7 = (bf16[2,64,320]{2,1,0:T(8,128)(2,1)S(1)}, bf16[2,64,320]{2,1,0:T(8,128)(2,1)S(1)}, u32[]{:S(2)}, u32[]{:S(2)}) collective-permute-start(bf16[2,64,320]{2,1,0:T(8,128)(2,1)S(1)} %get-tuple-element.123), channel_id=1, source_target_pairs={{0,24},{8,0},{16,8},{24,16},{1,25},{9,1},{17,9},{25,17},{2,26},{10... | collective-permute-start | bytes 245768 | tf_op jit(solution)/shard_map/ppermute | solution.py:559
  40.3 2.6 %collective-permute-done.6.refs_2_ = bf16[2,64,320]{2,1,0:T(8,128)(2,1)S(1)} collective-permute-done((bf16[2,64,320]{2,1,0:T(8,128)(2,1)S(1)}, bf16[2,64,320]{2,1,0:T(8,128)(2,1)S(1)}, u32[]{:S(2)}, u32[]{:S(2)}) %collective-permute-start.6) | collective-permute-done | bytes 81952 | tf_op jit(solution)/shard_map/ppermute | solution.py:559
  43.6 7.1 %collective-permute-start.11 = (bf16[2,64,320]{2,1,0:T(8,128)(2,1)S(1)}, bf16[2,64,320]{2,1,0:T(8,128)(2,1)S(1)}, u32[]{:S(2)}, u32[]{:S(2)}) collective-permute-start(bf16[2,64,320]{2,1,0:T(8,128)(2,1)S(1)} %get-tuple-element.135), channel_id=1, source_target_pairs={{0,24},{8,0},{16,8},{24,16},{1,25},{9,1},{17,9},{25,17},{2,26},{10... | collective-permute-start | bytes 245768 | tf_op jit(solution)/shard_map/ppermute | solution.py:568
  53.5 3.6 %shard_map.124 = (bf16[512,320]{1,0:T(8,128)(2,1)S(1)}, bf16[512,640]{1,0:T(8,128)(2,1)S(1)}, bf16[512,1920]{1,0:T(8,128)(2,1)S(1)}) custom-call(s32[4]{0:T(128)S(1)} %pad_add_fusion.info_ref.refs_0_, f32[512,320]{1,0:T(8,128)S(1)} %get-tuple-element.112.refs_1_, bf16[2,64,320]{2,1,0:T(8,128)(2,1)S(1)} %get-tuple-element.125.refs_2_, ...), custom_call_target="tpu_custom_call" | custom-call | flops 3000000000 | bytes 8765456 | tf_op jit(solution)/shard_map/pallas_call | solution.py:39
  57.0 3.9 %shard_map.125.refs_4_ = f32[16,640]{1,0:T(8,128)S(1)} custom-call(bf16[512,1920]{1,0:T(8,128)(2,1)S(1)} %get-tuple-element.130.refs_0_.left_a, bf16[1920,640]{1,0:T(8,128)(2,1)S(1)} %copy-done.2, f32[512,640]{1,0:T(8,128)S(1)} %get-tuple-element.131.refs_2_, f32[512,128]{1,0:T(8,128)S(1)} %get-tuple-element.132.refs_3_, ...), custom_call_target="tpu_custom_call" | custom-call | flops 5000000000 | bytes 7350784 | tf_op jit(solution)/shard_map/pallas_call | solution.py:39
  61.8 3.6 %shard_map.126 = (bf16[512,320]{1,0:T(8,128)(2,1)S(1)}, bf16[512,640]{1,0:T(8,128)(2,1)S(1)}, bf16[512,1920]{1,0:T(8,128)(2,1)S(1)}) custom-call(s32[4]{0:T(128)S(1)} %pad_add_fusion.info_ref.refs_0_, f32[512,320]{1,0:T(8,128)S(1)} %get-tuple-element.133.refs_1_, bf16[2,64,320]{2,1,0:T(8,128)(2,1)S(1)} %get-tuple-element.134.refs_2_, ...), custom_call_target="tpu_custom_call" | custom-call | flops 3000000000 | bytes 8765456 | tf_op jit(solution)/shard_map/pallas_call | solution.py:39
  65.4 3.9 %shard_map.127.refs_5_ = f32[16,640]{1,0:T(8,128)S(1)} custom-call(bf16[512,1920]{1,0:T(8,128)(2,1)S(1)} %get-tuple-element.157.refs_0_.left_b, bf16[1920,640]{1,0:T(8,128)(2,1)S(1)} %copy-done.2, f32[512,640]{1,0:T(8,128)S(1)} %get-tuple-element.145.refs_2_, f32[512,128]{1,0:T(8,128)S(1)} %get-tuple-element.146.refs_3_, ...), custom_call_target="tpu_custom_call" | custom-call | flops 5000000000 | bytes 8006144 | tf_op jit(solution)/shard_map/pallas_call | solution.py:39
  70.9 4.0 %shard_map.129 = (f32[16,64,640]{2,1,0:T(8,128)S(1)}, bf16[16,64,640]{2,1,0:T(8,128)(2,1)S(1)}) custom-call(s32[4]{0:T(128)S(1)} %pad_add_fusion.info_ref.refs_0_, bf16[512,1920]{1,0:T(8,128)(2,1)S(1)} %get-tuple-element.148.left_a, bf16[512,1920]{1,0:T(8,128)(2,1)S(1)} %get-tuple-element.149.left_b, bf16[512,640]{1,0:T(8,128)(2,1)S(1)} %get-tuple-element.150.right_a, ...), custom_call_target="tpu_custom_call" | custom-call | flops 6000000000 | bytes 9175056 | tf_op jit(solution)/shard_map/pallas_call | solution.py:39
  76.2 4.0 %shard_map.131 = (f32[16,64,640]{2,1,0:T(8,128)S(1)}, bf16[16,64,640]{2,1,0:T(8,128)(2,1)S(1)}) custom-call(s32[4]{0:T(128)S(1)} %pad_add_fusion.info_ref.refs_0_, bf16[512,1920]{1,0:T(8,128)(2,1)S(1)} %get-tuple-element.130.refs_0_.left_a, bf16[512,1920]{1,0:T(8,128)(2,1)S(1)} %get-tuple-element.157.refs_0_.left_b, ...), custom_call_target="tpu_custom_call" | custom-call | flops 6000000000 | bytes 9175056 | tf_op jit(solution)/shard_map/pallas_call | solution.py:39
  80.4 4.8 %collective-permute-start.15 = (bf16[8,16,640]{2,1,0:T(8,128)(2,1)S(1)}, bf16[8,16,640]{2,1,0:T(8,128)(2,1)S(1)}, u32[]{:S(2)}, u32[]{:S(2)}) collective-permute-start(bf16[8,16,640]{2,1,0:T(8,128)(2,1)S(1)} %get-tuple-element.164), channel_id=1, source_target_pairs={{0,2},{1,3},{2,0},{3,1},{4,6},{5,7},{6,4},{7,5},{8,10},{9,11},{10,... | collective-permute-start | bytes 491528 | tf_op jit(solution)/shard_map/ppermute | solution.py:423
  85.2 4.8 %collective-permute-done.15.refs_1_ = bf16[8,16,640]{2,1,0:T(8,128)(2,1)S(1)} collective-permute-done((bf16[8,16,640]{2,1,0:T(8,128)(2,1)S(1)}, bf16[8,16,640]{2,1,0:T(8,128)(2,1)S(1)}, u32[]{:S(2)}, u32[]{:S(2)}) %collective-permute-start.15) | collective-permute-done | bytes 163872 | tf_op jit(solution)/shard_map/ppermute | solution.py:423
  96.7 2.0 %collective-permute-start.18 = (bf16[4,16,640]{2,1,0:T(8,128)(2,1)S(1)}, bf16[4,16,640]{2,1,0:T(8,128)(2,1)S(1)}, u32[]{:S(2)}, u32[]{:S(2)}) collective-permute-start(bf16[4,16,640]{2,1,0:T(8,128)(2,1)S(1)} %get-tuple-element.175), channel_id=1, source_target_pairs={{0,4},{1,5},{2,6},{3,7},{4,0},{5,1},{6,2},{7,3},{8,12},{9,13},{10,... | collective-permute-start | bytes 245768 | tf_op jit(solution)/shard_map/ppermute | solution.py:423
  98.7 12.3 %collective-permute-done.18.got = bf16[4,16,640]{2,1,0:T(8,128)(2,1)S(1)} collective-permute-done((bf16[4,16,640]{2,1,0:T(8,128)(2,1)S(1)}, bf16[4,16,640]{2,1,0:T(8,128)(2,1)S(1)}, u32[]{:S(2)}, u32[]{:S(2)}) %collective-permute-start.18) | collective-permute-done | bytes 81952 | tf_op jit(solution)/shard_map/ppermute | solution.py:423
  111.8 2.0 %collective-permute-start.23 = (bf16[4,16,640]{2,1,0:T(8,128)(2,1)S(1)}, bf16[4,16,640]{2,1,0:T(8,128)(2,1)S(1)}, u32[]{:S(2)}, u32[]{:S(2)}) collective-permute-start(bf16[4,16,640]{2,1,0:T(8,128)(2,1)S(1)} %shard_map.135.refs_0_), channel_id=1, source_target_pairs={{0,8},{8,16},{16,24},{24,0},{1,9},{9,17},{17,25},{25,1},{2,10},{10... | collective-permute-start | bytes 245768 | tf_op jit(solution)/shard_map/ppermute | solution.py:476
  124.5 2.0 %collective-permute-done.29.refs_2_ = bf16[4,32,640]{2,1,0:T(8,128)(2,1)S(1)} collective-permute-done((bf16[4,32,640]{2,1,0:T(8,128)(2,1)S(1)}, bf16[4,32,640]{2,1,0:T(8,128)(2,1)S(1)}, u32[]{:S(2)}, u32[]{:S(2)}) %collective-permute-start.29) | collective-permute-done | bytes 163872 | tf_op jit(solution)/shard_map/ppermute | solution.py:423
  126.5 2.0 %collective-permute-done.30.refs_3_ = bf16[4,32,640]{2,1,0:T(8,128)(2,1)S(1)} collective-permute-done((bf16[4,32,640]{2,1,0:T(8,128)(2,1)S(1)}, bf16[4,32,640]{2,1,0:T(8,128)(2,1)S(1)}, u32[]{:S(2)}, u32[]{:S(2)}) %collective-permute-start.30) | collective-permute-done | bytes 163872 | tf_op jit(solution)/shard_map/ppermute | solution.py:423
  131.2 2.6 %collective-permute-start.36 = (bf16[64,640]{1,0:T(8,128)(2,1)S(1)}, bf16[64,640]{1,0:T(8,128)(2,1)S(1)}, u32[]{:S(2)}, u32[]{:S(2)}) collective-permute-start(bf16[64,640]{1,0:T(8,128)(2,1)S(1)} %get-tuple-element.209), channel_id=1, source_target_pairs={{0,24},{8,0},{16,8},{24,16},{1,25},{9,1},{17,9},{25,17},{2,26},{10... | collective-permute-start | bytes 245768 | tf_op jit(solution)/shard_map/ppermute | solution.py:433
  136.8 2.0 %collective-permute-start.33 = (bf16[64,640]{1,0:T(8,128)(2,1)S(1)}, bf16[64,640]{1,0:T(8,128)(2,1)S(1)}, u32[]{:S(2)}, u32[]{:S(2)}) collective-permute-start(bf16[64,640]{1,0:T(8,128)(2,1)S(1)} %get-tuple-element.205), channel_id=1, source_target_pairs={{0,24},{8,0},{16,8},{24,16},{1,25},{9,1},{17,9},{25,17},{2,26},{10... | collective-permute-start | bytes 245768 | tf_op jit(solution)/shard_map/ppermute | solution.py:433
  141.6 2.5 %collective-permute-done.32 = bf16[64,640]{1,0:T(8,128)(2,1)S(1)} collective-permute-done((bf16[64,640]{1,0:T(8,128)(2,1)S(1)}, bf16[64,640]{1,0:T(8,128)(2,1)S(1)}, u32[]{:S(2)}, u32[]{:S(2)}) %collective-permute-start.32) | collective-permute-done | bytes 81952 | tf_op jit(solution)/shard_map/ppermute | solution.py:433
  (106 shorter events, 51.6 us)
Async XLA Ops:
  4.2 19.5 %collective-permute-start = (bf16[2,1,128,640]{3,2,1,0:T(8,128)(2,1)S(1)}, bf16[2,1,128,640]{3,2,1,0:T(8,128)(2,1)S(1)}, u32[]{:S(2)}, u32[]{:S(2)}) collective-permute-start(bf16[2,1,128,640]{3,2,1,0:T(8,128)(2,1)S(1)} %get-tuple-element.109), channel_id=1, source_target_pairs={{0,1},{1,2},{2,3},{3,4},{4,5},{5,6},{6,7},{8,9},{9,10},{10,11},{11... | collective-permute-start | bytes 983048 | tf_op jit(solution)/shard_map/ppermute | solution.py:546
  6.6 17.1 %collective-permute-start.1 = (bf16[2,1,128,640]{3,2,1,0:T(8,128)(2,1)S(1)}, bf16[2,1,128,640]{3,2,1,0:T(8,128)(2,1)S(1)}, u32[]{:S(2)}, u32[]{:S(2)}) collective-permute-start(bf16[2,1,128,640]{3,2,1,0:T(8,128)(2,1)S(1)} %get-tuple-element.110), channel_id=1, source_target_pairs={{1,0},{2,1},{3,2},{4,3},{5,4},{6,5},{7,6},{9,8},{10,9},{11,10},{12... | collective-permute-start | bytes 983048 | tf_op jit(solution)/shard_map/ppermute | solution.py:547
  17.3 18.1 %collective-permute-start.2 = (bf16[2,64,320]{2,1,0:T(8,128)(2,1)S(1)}, bf16[2,64,320]{2,1,0:T(8,128)(2,1)S(1)}, u32[]{:S(2)}, u32[]{:S(2)}) collective-permute-start(bf16[2,64,320]{2,1,0:T(8,128)(2,1)S(1)} %get-tuple-element.114), channel_id=1, source_target_pairs={{0,8},{8,16},{16,24},{24,0},{1,9},{9,17},{17,25},{25,1},{2,10},{10... | collective-permute-start | bytes 245768 | tf_op jit(solution)/shard_map/ppermute | solution.py:559
  19.8 15.7 %collective-permute-start.3 = (bf16[2,64,320]{2,1,0:T(8,128)(2,1)S(1)}, bf16[2,64,320]{2,1,0:T(8,128)(2,1)S(1)}, u32[]{:S(2)}, u32[]{:S(2)}) collective-permute-start(bf16[2,64,320]{2,1,0:T(8,128)(2,1)S(1)} %get-tuple-element.115), channel_id=1, source_target_pairs={{0,16},{8,24},{16,0},{24,8},{1,17},{9,25},{17,1},{25,9},{2,18},{10... | collective-permute-start | bytes 245768 | tf_op jit(solution)/shard_map/ppermute | solution.py:559
  22.3 10.3 %collective-permute-start.4 = (bf16[2,64,320]{2,1,0:T(8,128)(2,1)S(1)}, bf16[2,64,320]{2,1,0:T(8,128)(2,1)S(1)}, u32[]{:S(2)}, u32[]{:S(2)}) collective-permute-start(bf16[2,64,320]{2,1,0:T(8,128)(2,1)S(1)} %get-tuple-element.116), channel_id=1, source_target_pairs={{0,24},{8,0},{16,8},{24,16},{1,25},{9,1},{17,9},{25,17},{2,26},{10... | collective-permute-start | bytes 245768 | tf_op jit(solution)/shard_map/ppermute | solution.py:559
  32.3 10.6 %collective-permute-start.6 = (bf16[2,64,320]{2,1,0:T(8,128)(2,1)S(1)}, bf16[2,64,320]{2,1,0:T(8,128)(2,1)S(1)}, u32[]{:S(2)}, u32[]{:S(2)}) collective-permute-start(bf16[2,64,320]{2,1,0:T(8,128)(2,1)S(1)} %get-tuple-element.122), channel_id=1, source_target_pairs={{0,16},{8,24},{16,0},{24,8},{1,17},{9,25},{17,1},{25,9},{2,18},{10... | collective-permute-start | bytes 245768 | tf_op jit(solution)/shard_map/ppermute | solution.py:559
  32.6 10.3 %collective-permute-start.7 = (bf16[2,64,320]{2,1,0:T(8,128)(2,1)S(1)}, bf16[2,64,320]{2,1,0:T(8,128)(2,1)S(1)}, u32[]{:S(2)}, u32[]{:S(2)}) collective-permute-start(bf16[2,64,320]{2,1,0:T(8,128)(2,1)S(1)} %get-tuple-element.123), channel_id=1, source_target_pairs={{0,24},{8,0},{16,8},{24,16},{1,25},{9,1},{17,9},{25,17},{2,26},{10... | collective-permute-start | bytes 245768 | tf_op jit(solution)/shard_map/ppermute | solution.py:559
  36.2 14.6 %collective-permute-start.8 = (bf16[2,64,320]{2,1,0:T(8,128)(2,1)S(1)}, bf16[2,64,320]{2,1,0:T(8,128)(2,1)S(1)}, u32[]{:S(2)}, u32[]{:S(2)}) collective-permute-start(bf16[2,64,320]{2,1,0:T(8,128)(2,1)S(1)} %get-tuple-element.126), channel_id=1, source_target_pairs={{0,24},{8,0},{16,8},{24,16},{1,25},{9,1},{17,9},{25,17},{2,26},{10... | collective-permute-start | bytes 245768 | tf_op jit(solution)/shard_map/ppermute | solution.py:568
  37.5 16.0 %collective-permute-start.9 = (bf16[2,64,320]{2,1,0:T(8,128)(2,1)S(1)}, bf16[2,64,320]{2,1,0:T(8,128)(2,1)S(1)}, u32[]{:S(2)}, u32[]{:S(2)}) collective-permute-start(bf16[2,64,320]{2,1,0:T(8,128)(2,1)S(1)} %get-tuple-element.127), channel_id=1, source_target_pairs={{0,16},{8,24},{16,0},{24,8},{1,17},{9,25},{17,1},{25,9},{2,18},{10... | collective-permute-start | bytes 245768 | tf_op jit(solution)/shard_map/ppermute | solution.py:568
  38.7 14.7 %collective-permute-start.10 = (bf16[2,64,320]{2,1,0:T(8,128)(2,1)S(1)}, bf16[2,64,320]{2,1,0:T(8,128)(2,1)S(1)}, u32[]{:S(2)}, u32[]{:S(2)}) collective-permute-start(bf16[2,64,320]{2,1,0:T(8,128)(2,1)S(1)} %get-tuple-element.128), channel_id=1, source_target_pairs={{0,8},{8,16},{16,24},{24,0},{1,9},{9,17},{17,25},{25,1},{2,10},{10... | collective-permute-start | bytes 245768 | tf_op jit(solution)/shard_map/ppermute | solution.py:568
  43.6 17.3 %collective-permute-start.11 = (bf16[2,64,320]{2,1,0:T(8,128)(2,1)S(1)}, bf16[2,64,320]{2,1,0:T(8,128)(2,1)S(1)}, u32[]{:S(2)}, u32[]{:S(2)}) collective-permute-start(bf16[2,64,320]{2,1,0:T(8,128)(2,1)S(1)} %get-tuple-element.135), channel_id=1, source_target_pairs={{0,24},{8,0},{16,8},{24,16},{1,25},{9,1},{17,9},{25,17},{2,26},{10... | collective-permute-start | bytes 245768 | tf_op jit(solution)/shard_map/ppermute | solution.py:568
  50.8 11.1 %collective-permute-start.12 = (bf16[2,64,320]{2,1,0:T(8,128)(2,1)S(1)}, bf16[2,64,320]{2,1,0:T(8,128)(2,1)S(1)}, u32[]{:S(2)}, u32[]{:S(2)}) collective-permute-start(bf16[2,64,320]{2,1,0:T(8,128)(2,1)S(1)} %get-tuple-element.136), channel_id=1, source_target_pairs={{0,16},{8,24},{16,0},{24,8},{1,17},{9,25},{17,1},{25,9},{2,18},{10... | collective-permute-start | bytes 245768 | tf_op jit(solution)/shard_map/ppermute | solution.py:568
  50.8 11.1 %collective-permute-start.13 = (bf16[2,64,320]{2,1,0:T(8,128)(2,1)S(1)}, bf16[2,64,320]{2,1,0:T(8,128)(2,1)S(1)}, u32[]{:S(2)}, u32[]{:S(2)}) collective-permute-start(bf16[2,64,320]{2,1,0:T(8,128)(2,1)S(1)} %get-tuple-element.137), channel_id=1, source_target_pairs={{0,8},{8,16},{16,24},{24,0},{1,9},{9,17},{17,25},{25,1},{2,10},{10... | collective-permute-start | bytes 245768 | tf_op jit(solution)/shard_map/ppermute | solution.py:568
  74.9 15.8 %collective-permute-start.16 = (bf16[16,64,640]{2,1,0:T(8,128)(2,1)S(1)}, bf16[16,64,640]{2,1,0:T(8,128)(2,1)S(1)}, u32[]{:S(2)}, u32[]{:S(2)}) collective-permute-start(bf16[16,64,640]{2,1,0:T(8,128)(2,1)S(1)} %get-tuple-element.167), channel_id=1, source_target_pairs={{0,1},{1,0},{2,3},{3,2},{4,5},{5,4},{6,7},{7,6},{8,9},{9,8},{10,11... | collective-permute-start | bytes 3932168 | tf_op jit(solution)/shard_map/ppermute | solution.py:403
  80.2 14.1 %collective-permute-start.17 = (bf16[16,64,640]{2,1,0:T(8,128)(2,1)S(1)}, bf16[16,64,640]{2,1,0:T(8,128)(2,1)S(1)}, u32[]{:S(2)}, u32[]{:S(2)}) collective-permute-start(bf16[16,64,640]{2,1,0:T(8,128)(2,1)S(1)} %get-tuple-element.172), channel_id=1, source_target_pairs={{0,1},{1,0},{2,3},{3,2},{4,5},{5,4},{6,7},{7,6},{8,9},{9,8},{10,11... | collective-permute-start | bytes 3932168 | tf_op jit(solution)/shard_map/ppermute | solution.py:403
  80.4 9.6 %collective-permute-start.15 = (bf16[8,16,640]{2,1,0:T(8,128)(2,1)S(1)}, bf16[8,16,640]{2,1,0:T(8,128)(2,1)S(1)}, u32[]{:S(2)}, u32[]{:S(2)}) collective-permute-start(bf16[8,16,640]{2,1,0:T(8,128)(2,1)S(1)} %get-tuple-element.164), channel_id=1, source_target_pairs={{0,2},{1,3},{2,0},{3,1},{4,6},{5,7},{6,4},{7,5},{8,10},{9,11},{10,... | collective-permute-start | bytes 491528 | tf_op jit(solution)/shard_map/ppermute | solution.py:423
  91.5 20.1 %collective-permute-start.19 = (bf16[8,32,640]{2,1,0:T(8,128)(2,1)S(1)}, bf16[8,32,640]{2,1,0:T(8,128)(2,1)S(1)}, u32[]{:S(2)}, u32[]{:S(2)}) collective-permute-start(bf16[8,32,640]{2,1,0:T(8,128)(2,1)S(1)} %get-tuple-element.180), channel_id=1, source_target_pairs={{0,2},{1,3},{2,0},{3,1},{4,6},{5,7},{6,4},{7,5},{8,10},{9,11},{10,... | collective-permute-start | bytes 983048 | tf_op jit(solution)/shard_map/ppermute | solution.py:423
  93.3 18.4 %collective-permute-start.20 = (bf16[8,32,640]{2,1,0:T(8,128)(2,1)S(1)}, bf16[8,32,640]{2,1,0:T(8,128)(2,1)S(1)}, u32[]{:S(2)}, u32[]{:S(2)}) collective-permute-start(bf16[8,32,640]{2,1,0:T(8,128)(2,1)S(1)} %get-tuple-element.181), channel_id=1, source_target_pairs={{0,4},{1,5},{2,6},{3,7},{4,0},{5,1},{6,2},{7,3},{8,12},{9,13},{10,... | collective-permute-start | bytes 983048 | tf_op jit(solution)/shard_map/ppermute | solution.py:423
  95.2 19.2 %collective-permute-start.21 = (bf16[8,32,640]{2,1,0:T(8,128)(2,1)S(1)}, bf16[8,32,640]{2,1,0:T(8,128)(2,1)S(1)}, u32[]{:S(2)}, u32[]{:S(2)}) collective-permute-start(bf16[8,32,640]{2,1,0:T(8,128)(2,1)S(1)} %get-tuple-element.186), channel_id=1, source_target_pairs={{0,2},{1,3},{2,0},{3,1},{4,6},{5,7},{6,4},{7,5},{8,10},{9,11},{10,... | collective-permute-start | bytes 983048 | tf_op jit(solution)/shard_map/ppermute | solution.py:423
  96.7 18.8 %collective-permute-start.22 = (bf16[8,32,640]{2,1,0:T(8,128)(2,1)S(1)}, bf16[8,32,640]{2,1,0:T(8,128)(2,1)S(1)}, u32[]{:S(2)}, u32[]{:S(2)}) collective-permute-start(bf16[8,32,640]{2,1,0:T(8,128)(2,1)S(1)} %get-tuple-element.187), channel_id=1, source_target_pairs={{0,4},{1,5},{2,6},{3,7},{4,0},{5,1},{6,2},{7,3},{8,12},{9,13},{10,... | collective-permute-start | bytes 983048 | tf_op jit(solution)/shard_map/ppermute | solution.py:423
  96.7 14.3 %collective-permute-start.18 = (bf16[4,16,640]{2,1,0:T(8,128)(2,1)S(1)}, bf16[4,16,640]{2,1,0:T(8,128)(2,1)S(1)}, u32[]{:S(2)}, u32[]{:S(2)}) collective-permute-start(bf16[4,16,640]{2,1,0:T(8,128)(2,1)S(1)} %get-tuple-element.175), channel_id=1, source_target_pairs={{0,4},{1,5},{2,6},{3,7},{4,0},{5,1},{6,2},{7,3},{8,12},{9,13},{10,... | collective-permute-start | bytes 245768 | tf_op jit(solution)/shard_map/ppermute | solution.py:423
  114.5 8.4 %collective-permute-start.27 = (bf16[4,32,640]{2,1,0:T(8,128)(2,1)S(1)}, bf16[4,32,640]{2,1,0:T(8,128)(2,1)S(1)}, u32[]{:S(2)}, u32[]{:S(2)}) collective-permute-start(bf16[4,32,640]{2,1,0:T(8,128)(2,1)S(1)} %get-tuple-element.194), channel_id=1, source_target_pairs={{0,4},{1,5},{2,6},{3,7},{4,0},{5,1},{6,2},{7,3},{8,12},{9,13},{10,... | collective-permute-start | bytes 491528 | tf_op jit(solution)/shard_map/ppermute | solution.py:423
  130.0 9.2 %collective-permute-start.35 = (bf16[64,640]{1,0:T(8,128)(2,1)S(1)}, bf16[64,640]{1,0:T(8,128)(2,1)S(1)}, u32[]{:S(2)}, u32[]{:S(2)}) collective-permute-start(bf16[64,640]{1,0:T(8,128)(2,1)S(1)} %get-tuple-element.208), channel_id=1, source_target_pairs={{0,16},{8,24},{16,0},{24,8},{1,17},{9,25},{17,1},{25,9},{2,18},{10... | collective-permute-start | bytes 245768 | tf_op jit(solution)/shard_map/ppermute | solution.py:433
  134.5 9.5 %collective-permute-start.32 = (bf16[64,640]{1,0:T(8,128)(2,1)S(1)}, bf16[64,640]{1,0:T(8,128)(2,1)S(1)}, u32[]{:S(2)}, u32[]{:S(2)}) collective-permute-start(bf16[64,640]{1,0:T(8,128)(2,1)S(1)} %get-tuple-element.204), channel_id=1, source_target_pairs={{0,16},{8,24},{16,0},{24,8},{1,17},{9,25},{17,1},{25,9},{2,18},{10... | collective-permute-start | bytes 245768 | tf_op jit(solution)/shard_map/ppermute | solution.py:433
  (24 other events, 130.3 us)
where the time goes:
time: 148 us
  starting transfers between devices  54.1 us (37%)
  Pallas kernels  49.7 us (34%)
  waiting for transfers between devices  34.9 us (24%)
  local copies, waits for them, and re-layouts  6.53 us (4%)
  other arithmetic  1.62 us (1%)
    pallas_call x23, Pallas kernels, call(): pl.pallas_call(kernel, in_specs=[SMEM] * scalars + [pl.BlockSpec(memory_s...  49.7 us
    ppermute x10, waiting for transfers between devices, merge_blocks(): lax.ppermute(part, 'space', flip(spaces, 1 << order[depth]))  21.1 us
    ppermute x10, starting transfers between devices, merge_blocks(): lax.ppermute(part, 'space', flip(spaces, 1 << order[depth]))  15.4 us
    ppermute x6, starting transfers between devices, body(): lax.ppermute(pulls[k], 'member', ring(members, members - k))  11.9 us
    ppermute x6, starting transfers between devices, body(): lax.ppermute(sends[k], 'member', ring(members, k))  10.4 us
    ppermute x6, starting transfers between devices, turn_blocks(): lax.ppermute(parts[k], 'member', ring(members, k))  7.69 us
    ppermute x6, waiting for transfers between devices, turn_blocks(): lax.ppermute(parts[k], 'member', ring(members, k))  5.5 us
    unnamed x19, local copies, waits for them, and re-layouts  4.89 us
  transfers between devices with their start and end apart: 39, of which 17 were waited for; matrix products, arithmetic and copies ran while one was open for 1% of the time, Pallas kernels for 26%

commit v1 on v0

--- a/solution.py
+++ b/solution.py
@@ -199,13 +199,10 @@
             grad[at, :] = (scale * (attract[at, :] - pulls[k][m].astype(F32) * share)).astype(BF16)
     ghid[...] = dot(grad[...], w_head[...]).astype(BF16)
 
-    def unit_step(t, carry):
-        at = pl.ds(pl.multiple_of(t * tile, tile), tile)
+    for t in range(w_down.shape[0] // tile):
+        at = pl.ds(t * tile, tile)
         back = dot(ghid[...], w_down[at, :], LAST)
         gpre[:, at] = (slope[:, at].astype(F32) * back).astype(BF16)
-        return carry
-
-    lax.fori_loop(0, w_down.shape[0] // tile, unit_step, 0)
 
 
 def slopes(me, attract, pulls, w_head, w_down, slope, scale, share):
@@ -460,14 +457,24 @@
     return sum(((index >> b) & 1) << (bits - 1 - b) for b in range(bits))
 
 
-def place_kernel(info_ref, rel, out):
+def place_kernel(info_ref, rel, head, conv, gain, hold):
     spaces, members = rel.shape[:2]
     place = 0
     for bit in range(spaces.bit_length() - 1):
         place = place + info_ref[1 + bit] * (1 << bit)
     for r in range(spaces):
         for m in range(members):
-            out[m * spaces + (place ^ turned(r, spaces))] = rel[r, m].astype(F32)
+            hold[m * spaces + (place ^ turned(r, spaces))] = rel[r, m].astype(F32)
+    wide = head.shape[0]
+    rows = -(-wide // (members * spaces))
+    for block in range(members * spaces):
+        size = min(rows, wide - block * rows)
+        if size > 0:
+            head[block * rows : block * rows + size, :] = hold[block, 0:size, :]
+        if block < SMALL - 1:
+            conv[block : block + 1, :] = hold[block, rows : rows + 1, :]
+        elif block == SMALL - 1:
+            gain[...] = hold[block, rows : rows + 1, :]
 
 
 def fold_members(info, keep, got):
@@ -486,10 +493,12 @@
     return jnp.concatenate([whole, other], axis=0)
 
 
-def placed(info, whole):
+def placed(info, whole, wide):
     spaces, members = whole.shape[:2]
-    outs = [((members * spaces,) + whole.shape[2:], F32)]
-    return call(place_kernel, [info, whole], outs, [], 1)[0]
+    width = whole.shape[3]
+    outs = [((wide, width), F32), ((SMALL - 1, width), F32), ((1, width), F32)]
+    scratch = [pltpu.VMEM((members * spaces,) + whole.shape[2:], F32)]
+    return call(place_kernel, [info, whole], outs, scratch, 1)
 
 
 def after(value, other):
@@ -512,7 +521,7 @@
     mem_dev, _, lon, width = noise.shape
     edge = ((mem_dev, 1, lon, width), BF16)
     outs = [(noise.shape, BF16), edge, edge]
-    return call(mix_kernel, [info, latent, noise], outs, [], 1)
+    return call(mix_kernel, [info, latent, noise], outs, [], 20)
 
 
 def body(
@@ -578,13 +587,16 @@
         grads.append(
             slopes(info, attract, backs[half], head_t, weight_down, slope, scale, share)
         )
-        smalls.append(
-            norms(
-                grads[half][2], weight_in, normal, inv, gain, mixed, edges, rows,
+        if half == 0:
+            smalls.append(
+                norms(grads[0][2], weight_in, normal, inv, gain, mixed, edges, rows)
             )
-        )
 
     hids = [saved[h][5] for h in range(2)]
+    depths = spaces.bit_length() - 2
+    rows, edges = halves[1]
+    normal, inv = saved[1][1:3]
+    smalls.append(norms(grads[1][2], weight_in, normal, inv, gain, mixed, edges, rows))
     keep_h, send_h = heads(info, [grads[h][0] for h in range(2)], hids, smalls, devices)
     got_h = start_blocks(send_h)
     keep_d, send_d = weights(
@@ -599,7 +611,6 @@
     keep_i, send_i = weights(info, gpre, [saved[h][0] for h in range(2)], devices)
     got_i = start_blocks(send_i)
     part_h[0][0], keep_i = after(part_h[0][0], keep_i)
-    depths = spaces.bit_length() - 2
     for depth in range(1, depths):
         part_h = merge_blocks(info, *part_h, flows_h, depth)
     keep_d, part_h[0][0] = after(keep_d, part_h[0][0])
@@ -613,28 +624,28 @@
     part_d[0][0], own_h = after(part_d[0][0], own_h)
     for depth in range(1, depths):
         part_d = merge_blocks(info, *part_d, flows_d, depth)
-        part_i[0][0], part_d[0][0] = after(part_i[0][0], part_d[0][0])
-        part_i = merge_blocks(info, *part_i, flows_d, depth)
-        part_d[0][0], part_i[0][0] = after(part_d[0][0], part_i[0][0])
-    own_h, part_i[0][0] = after(own_h, part_i[0][0])
+    own_h, part_d[0][0] = after(own_h, part_d[0][0])
     whole = fold(info, [own_h, *others_h])[None]
     bit = spaces // 2
+    part_i[0][0], whole = after(part_i[0][0], whole)
     whole = spread_step(whole, bit)
+    for depth in range(1, depths):
+        part_i = merge_blocks(info, *part_i, flows_d, depth)
+    part_d[0][0], part_i[0][0] = after(part_d[0][0], part_i[0][0])
     own_d, others_d = turn_blocks(info, *part_d)
     part_i[0][0], own_d = after(part_i[0][0], own_d)
+    whole, own_d = after(whole, own_d)
+    while bit > 2:
+        bit //= 2
+        whole = spread_step(whole, bit)
     own_i, others_i = turn_blocks(info, *part_i)
     whole, own_i = after(whole, own_i)
-    while bit > 1:
-        bit //= 2
-        whole = spread_step(whole, bit)
-    gathered = placed(info, whole)
+    whole = spread_step(whole, 1)
     units = weight_in.shape[0] // devices
-    head_rows = -(-out_width // devices)
-    head_total = gathered[:, :head_rows].reshape(-1, width)[:out_width].T
-    small = gathered[:SMALL, head_rows]
+    head_total, conv_total, gain_total = placed(info, whole, out_width)
     in_mine = add_up(own_i, others_i)[:units]
     down_mine = add_up(own_d, others_d)[:units]
-    return (in_mine, down_mine, head_total, small[9], small[:9])
+    return (in_mine, down_mine, head_total.T, gain_total.reshape(width), conv_total)
 
 
 def solution(mesh):

time: 148 us -> 139 us (0.939)
  waiting for transfers between devices: 34.9 us -> 29 us
  local copies, waits for them, and re-layouts: 6.53 us -> 2.44 us
    ppermute x10, waiting for transfers between devices: 21.1 us -> 13.2 us  [merge_blocks(): lax.ppermute(part, 'space', flip(spaces, 1 << order[depth]))]
    unnamed x19 -> x16, local copies, waits for them, and re-layouts: 4.89 us -> 2.43 us
  transfers between devices with their start and end apart: 39 -> 39, of which waited for: 17 -> 13; matrix products, arithmetic and copies ran while one was open for 1% -> 1% of each run, Pallas kernels for 26% -> 28%
where the time goes in v1:
time: 139 us
  starting transfers between devices  54.9 us (39%)
  Pallas kernels  49.4 us (36%)
  waiting for transfers between devices  29 us (21%)
  local copies, waits for them, and re-layouts  2.44 us (2%)
  other arithmetic  2.23 us (2%)
    pallas_call x23, Pallas kernels, call(): pl.pallas_call(kernel, in_specs=[SMEM] * scalars + [pl.BlockSpec(memory_s...  49.4 us
    ppermute x10, starting transfers between devices, merge_blocks(): lax.ppermute(part, 'space', flip(spaces, 1 << order[depth]))  14.2 us
    ppermute x10, waiting for transfers between devices, merge_blocks(): lax.ppermute(part, 'space', flip(spaces, 1 << order[depth]))  13.2 us
    ppermute x6, starting transfers between devices, body(): lax.ppermute(pulls[k], 'member', ring(members, members - k))  11.9 us
    ppermute x6, starting transfers between devices, body(): lax.ppermute(sends[k], 'member', ring(members, k))  10.4 us
    ppermute x6, starting transfers between devices, turn_blocks(): lax.ppermute(parts[k], 'member', ring(members, k))  8.99 us
    ppermute x6, waiting for transfers between devices, turn_blocks(): lax.ppermute(parts[k], 'member', ring(members, k))  4.61 us
    ppermute x6, waiting for transfers between devices, body(): lax.ppermute(pulls[k], 'member', ring(members, members - k))  3.15 us
  transfers between devices with their start and end apart: 39, of which 13 were waited for; matrix products, arithmetic and copies ran while one was open for 1% of the time, Pallas kernels for 28%

profile of v1, /device:TPU:0, one launch (start us, length us, event | category | flops | bytes accessed | tf_op | source)
XLA Modules:
  0.0 139.0 jit_solution(12974330375512667852)
XLA Ops:
  4.0 2.7 %collective-permute-start.3 = (bf16[2,1,128,640]{3,2,1,0:T(8,128)(2,1)S(1)}, bf16[2,1,128,640]{3,2,1,0:T(8,128)(2,1)S(1)}, u32[]{:S(2)}, u32[]{:S(2)}) collective-permute-start(bf16[2,1,128,640]{3,2,1,0:T(8,128)(2,1)S(1)} %get-tuple-element.119), channel_id=1, source_target_pairs={{0,1},{1,2},{2,3},{3,4},{4,5},{5,6},{6,7},{8,9},{9,10},{10,11},{11... | collective-permute-start | bytes 983048 | tf_op jit(solution)/shard_map/ppermute | solution.py:555
  8.1 7.7 %shard_map.120 = (bf16[512,640]{1,0:T(8,128)(2,1)S(1)}, f32[512,640]{1,0:T(8,128)S(1)}, f32[512,128]{1,0:T(8,128)S(1)}, bf16[512,1920]{1,0:T(8,128)(2,1)S(1)}, b...) custom-call(s32[4]{0:T(128)S(1)} %pad_add_fusion.info_ref.refs_0_, ...), custom_call_target="tpu_custom_call" | custom-call | flops 8999999488 | bytes 15115280 | tf_op jit(solution)/shard_map/pallas_call | solution.py:39
  15.8 2.4 %collective-permute-start = (bf16[2,64,320]{2,1,0:T(8,128)(2,1)S(1)}, bf16[2,64,320]{2,1,0:T(8,128)(2,1)S(1)}, u32[]{:S(2)}, u32[]{:S(2)}) collective-permute-start(bf16[2,64,320]{2,1,0:T(8,128)(2,1)S(1)} %get-tuple-element.116), channel_id=1, source_target_pairs={{0,8},{8,16},{16,24},{24,0},{1,9},{9,17},{17,25},{25,1},{2,10},{10... | collective-permute-start | bytes 245768 | tf_op jit(solution)/shard_map/ppermute | solution.py:568
  18.2 2.6 %collective-permute-start.1 = (bf16[2,64,320]{2,1,0:T(8,128)(2,1)S(1)}, bf16[2,64,320]{2,1,0:T(8,128)(2,1)S(1)}, u32[]{:S(2)}, u32[]{:S(2)}) collective-permute-start(bf16[2,64,320]{2,1,0:T(8,128)(2,1)S(1)} %get-tuple-element.117), channel_id=1, source_target_pairs={{0,16},{8,24},{16,0},{24,8},{1,17},{9,25},{17,1},{25,9},{2,18},{10... | collective-permute-start | bytes 245768 | tf_op jit(solution)/shard_map/ppermute | solution.py:568
  22.1 7.6 %shard_map.121 = (bf16[512,640]{1,0:T(8,128)(2,1)S(1)}, f32[512,640]{1,0:T(8,128)S(1)}, f32[512,128]{1,0:T(8,128)S(1)}, bf16[512,1920]{1,0:T(8,128)(2,1)S(1)}, b...) custom-call(s32[4]{0:T(128)S(1)} %pad_add_fusion.info_ref.refs_0_, ...), custom_call_target="tpu_custom_call" | custom-call | flops 8999999488 | bytes 15770640 | tf_op jit(solution)/shard_map/pallas_call | solution.py:39
  31.0 2.8 %collective-permute-start.7 = (bf16[2,64,320]{2,1,0:T(8,128)(2,1)S(1)}, bf16[2,64,320]{2,1,0:T(8,128)(2,1)S(1)}, u32[]{:S(2)}, u32[]{:S(2)}) collective-permute-start(bf16[2,64,320]{2,1,0:T(8,128)(2,1)S(1)} %get-tuple-element.127), channel_id=1, source_target_pairs={{0,24},{8,0},{16,8},{24,16},{1,25},{9,1},{17,9},{25,17},{2,26},{10... | collective-permute-start | bytes 245768 | tf_op jit(solution)/shard_map/ppermute | solution.py:568
  38.7 2.6 %collective-permute-done.6.refs_2_ = bf16[2,64,320]{2,1,0:T(8,128)(2,1)S(1)} collective-permute-done((bf16[2,64,320]{2,1,0:T(8,128)(2,1)S(1)}, bf16[2,64,320]{2,1,0:T(8,128)(2,1)S(1)}, u32[]{:S(2)}, u32[]{:S(2)}) %collective-permute-start.6) | collective-permute-done | bytes 81952 | tf_op jit(solution)/shard_map/ppermute | solution.py:568
  42.0 7.1 %collective-permute-start.11 = (bf16[2,64,320]{2,1,0:T(8,128)(2,1)S(1)}, bf16[2,64,320]{2,1,0:T(8,128)(2,1)S(1)}, u32[]{:S(2)}, u32[]{:S(2)}) collective-permute-start(bf16[2,64,320]{2,1,0:T(8,128)(2,1)S(1)} %get-tuple-element.141), channel_id=1, source_target_pairs={{0,24},{8,0},{16,8},{24,16},{1,25},{9,1},{17,9},{25,17},{2,26},{10... | collective-permute-start | bytes 245768 | tf_op jit(solution)/shard_map/ppermute | solution.py:577
  51.9 3.0 %shard_map.124 = (bf16[512,320]{1,0:T(8,128)(2,1)S(1)}, bf16[512,640]{1,0:T(8,128)(2,1)S(1)}, bf16[512,1920]{1,0:T(8,128)(2,1)S(1)}) custom-call(s32[4]{0:T(128)S(1)} %pad_add_fusion.info_ref.refs_0_, f32[512,320]{1,0:T(8,128)S(1)} %get-tuple-element.114.refs_1_, bf16[2,64,320]{2,1,0:T(8,128)(2,1)S(1)} %get-tuple-element.129.refs_2_, ...), custom_call_target="tpu_custom_call" | custom-call | flops 3000000000 | bytes 8765456 | tf_op jit(solution)/shard_map/pallas_call | solution.py:39
  54.8 3.9 %shard_map.125.refs_4_ = f32[16,640]{1,0:T(8,128)S(1)} custom-call(bf16[512,1920]{1,0:T(8,128)(2,1)S(1)} %get-tuple-element.136.refs_0_.left_a, bf16[1920,640]{1,0:T(8,128)(2,1)S(1)} %copy-done.1, f32[512,640]{1,0:T(8,128)S(1)} %get-tuple-element.137.refs_2_, f32[512,128]{1,0:T(8,128)S(1)} %get-tuple-element.138.refs_3_, ...), custom_call_target="tpu_custom_call" | custom-call | flops 5000000000 | bytes 7350784 | tf_op jit(solution)/shard_map/pallas_call | solution.py:39
  60.2 3.0 %shard_map.126 = (bf16[512,320]{1,0:T(8,128)(2,1)S(1)}, bf16[512,640]{1,0:T(8,128)(2,1)S(1)}, bf16[512,1920]{1,0:T(8,128)(2,1)S(1)}) custom-call(s32[4]{0:T(128)S(1)} %pad_add_fusion.info_ref.refs_0_, f32[512,320]{1,0:T(8,128)S(1)} %get-tuple-element.139.refs_1_, bf16[2,64,320]{2,1,0:T(8,128)(2,1)S(1)} %get-tuple-element.140.refs_2_, ...), custom_call_target="tpu_custom_call" | custom-call | flops 3000000000 | bytes 8765456 | tf_op jit(solution)/shard_map/pallas_call | solution.py:39
  63.2 3.9 %shard_map.127.refs_5_ = f32[16,640]{1,0:T(8,128)S(1)} custom-call(bf16[512,1920]{1,0:T(8,128)(2,1)S(1)} %get-tuple-element.163.refs_0_.left_b, bf16[1920,640]{1,0:T(8,128)(2,1)S(1)} %copy-done.1, f32[512,640]{1,0:T(8,128)S(1)} %get-tuple-element.150.refs_2_, f32[512,128]{1,0:T(8,128)S(1)} %get-tuple-element.151.refs_3_, ...), custom_call_target="tpu_custom_call" | custom-call | flops 5000000000 | bytes 8006144 | tf_op jit(solution)/shard_map/pallas_call | solution.py:39
  68.7 4.0 %shard_map.129 = (f32[16,64,640]{2,1,0:T(8,128)S(1)}, bf16[16,64,640]{2,1,0:T(8,128)(2,1)S(1)}) custom-call(s32[4]{0:T(128)S(1)} %pad_add_fusion.info_ref.refs_0_, bf16[512,1920]{1,0:T(8,128)(2,1)S(1)} %get-tuple-element.153.left_a, bf16[512,1920]{1,0:T(8,128)(2,1)S(1)} %get-tuple-element.154.left_b, bf16[512,640]{1,0:T(8,128)(2,1)S(1)} %get-tuple-element.155.right_a, ...), custom_call_target="tpu_custom_call" | custom-call | flops 6000000000 | bytes 9175056 | tf_op jit(solution)/shard_map/pallas_call | solution.py:39
  74.0 4.0 %shard_map.131 = (f32[16,64,640]{2,1,0:T(8,128)S(1)}, bf16[16,64,640]{2,1,0:T(8,128)(2,1)S(1)}) custom-call(s32[4]{0:T(128)S(1)} %pad_add_fusion.info_ref.refs_0_, bf16[512,1920]{1,0:T(8,128)(2,1)S(1)} %get-tuple-element.136.refs_0_.left_a, bf16[512,1920]{1,0:T(8,128)(2,1)S(1)} %get-tuple-element.163.refs_0_.left_b, ...), custom_call_target="tpu_custom_call" | custom-call | flops 6000000000 | bytes 9175056 | tf_op jit(solution)/shard_map/pallas_call | solution.py:39
  78.2 4.2 %collective-permute-start.15 = (bf16[8,16,640]{2,1,0:T(8,128)(2,1)S(1)}, bf16[8,16,640]{2,1,0:T(8,128)(2,1)S(1)}, u32[]{:S(2)}, u32[]{:S(2)}) collective-permute-start(bf16[8,16,640]{2,1,0:T(8,128)(2,1)S(1)} %get-tuple-element.168), channel_id=1, source_target_pairs={{0,2},{1,3},{2,0},{3,1},{4,6},{5,7},{6,4},{7,5},{8,10},{9,11},{10,... | collective-permute-start | bytes 491528 | tf_op jit(solution)/shard_map/ppermute | solution.py:420
  82.4 4.8 %collective-permute-done.15.refs_1_ = bf16[8,16,640]{2,1,0:T(8,128)(2,1)S(1)} collective-permute-done((bf16[8,16,640]{2,1,0:T(8,128)(2,1)S(1)}, bf16[8,16,640]{2,1,0:T(8,128)(2,1)S(1)}, u32[]{:S(2)}, u32[]{:S(2)}) %collective-permute-start.15) | collective-permute-done | bytes 163872 | tf_op jit(solution)/shard_map/ppermute | solution.py:420
  88.7 1.8 %collective-permute-start.19 = (bf16[8,32,640]{2,1,0:T(8,128)(2,1)S(1)}, bf16[8,32,640]{2,1,0:T(8,128)(2,1)S(1)}, u32[]{:S(2)}, u32[]{:S(2)}) collective-permute-start(bf16[8,32,640]{2,1,0:T(8,128)(2,1)S(1)} %get-tuple-element.185), channel_id=1, source_target_pairs={{0,2},{1,3},{2,0},{3,1},{4,6},{5,7},{6,4},{7,5},{8,10},{9,11},{10,... | collective-permute-start | bytes 983048 | tf_op jit(solution)/shard_map/ppermute | solution.py:420
  93.4 7.7 %collective-permute-done.18.got = bf16[4,16,640]{2,1,0:T(8,128)(2,1)S(1)} collective-permute-done((bf16[4,16,640]{2,1,0:T(8,128)(2,1)S(1)}, bf16[4,16,640]{2,1,0:T(8,128)(2,1)S(1)}, u32[]{:S(2)}, u32[]{:S(2)}) %collective-permute-start.18) | collective-permute-done | bytes 81952 | tf_op jit(solution)/shard_map/ppermute | solution.py:420
  101.9 1.9 %collective-permute-start.21 = (bf16[4,16,640]{2,1,0:T(8,128)(2,1)S(1)}, bf16[4,16,640]{2,1,0:T(8,128)(2,1)S(1)}, u32[]{:S(2)}, u32[]{:S(2)}) collective-permute-start(bf16[4,16,640]{2,1,0:T(8,128)(2,1)S(1)} %shard_map.135.refs_0_), channel_id=1, source_target_pairs={{0,8},{8,16},{16,24},{24,0},{1,9},{9,17},{17,25},{25,1},{2,10},{10... | collective-permute-start | bytes 245768 | tf_op jit(solution)/shard_map/ppermute | solution.py:483
  113.1 2.6 %collective-permute-done.24 = bf16[1,4,16,640]{3,2,1,0:T(8,128)(2,1)S(1)} collective-permute-done((bf16[1,4,16,640]{3,2,1,0:T(8,128)(2,1)S(1)}, bf16[1,4,16,640]{3,2,1,0:T(8,128)(2,1)S(1)}, u32[]{:S(2)}, u32[]{:S(2)}) %collective-permute-start.24) | collective-permute-done | bytes 81952 | tf_op jit(solution)/shard_map/ppermute | solution.py:492
  116.4 1.8 %collective-permute-start.30 = (bf16[4,32,640]{2,1,0:T(8,128)(2,1)S(1)}, bf16[4,32,640]{2,1,0:T(8,128)(2,1)S(1)}, u32[]{:S(2)}, u32[]{:S(2)}) collective-permute-start(bf16[4,32,640]{2,1,0:T(8,128)(2,1)S(1)} %get-tuple-element.206), channel_id=1, source_target_pairs={{0,4},{1,5},{2,6},{3,7},{4,0},{5,1},{6,2},{7,3},{8,12},{9,13},{10,... | collective-permute-start | bytes 491528 | tf_op jit(solution)/shard_map/ppermute | solution.py:420
  123.7 2.4 %collective-permute-start.37 = (bf16[64,640]{1,0:T(8,128)(2,1)S(1)}, bf16[64,640]{1,0:T(8,128)(2,1)S(1)}, u32[]{:S(2)}, u32[]{:S(2)}) collective-permute-start(bf16[64,640]{1,0:T(8,128)(2,1)S(1)} %get-tuple-element.216), channel_id=1, source_target_pairs={{0,24},{8,0},{16,8},{24,16},{1,25},{9,1},{17,9},{25,17},{2,26},{10... | collective-permute-start | bytes 245768 | tf_op jit(solution)/shard_map/ppermute | solution.py:430
  128.2 2.5 %collective-permute-start.34 = (bf16[64,640]{1,0:T(8,128)(2,1)S(1)}, bf16[64,640]{1,0:T(8,128)(2,1)S(1)}, u32[]{:S(2)}, u32[]{:S(2)}) collective-permute-start(bf16[64,640]{1,0:T(8,128)(2,1)S(1)} %get-tuple-element.212), channel_id=1, source_target_pairs={{0,24},{8,0},{16,8},{24,16},{1,25},{9,1},{17,9},{25,17},{2,26},{10... | collective-permute-start | bytes 245768 | tf_op jit(solution)/shard_map/ppermute | solution.py:430
  133.1 2.9 %collective-permute-done.33 = bf16[64,640]{1,0:T(8,128)(2,1)S(1)} collective-permute-done((bf16[64,640]{1,0:T(8,128)(2,1)S(1)}, bf16[64,640]{1,0:T(8,128)(2,1)S(1)}, u32[]{:S(2)}, u32[]{:S(2)}) %collective-permute-start.33) | collective-permute-done | bytes 81952 | tf_op jit(solution)/shard_map/ppermute | solution.py:430
  (101 shorter events, 48.2 us)
Async XLA Ops:
  4.0 18.1 %collective-permute-start.3 = (bf16[2,1,128,640]{3,2,1,0:T(8,128)(2,1)S(1)}, bf16[2,1,128,640]{3,2,1,0:T(8,128)(2,1)S(1)}, u32[]{:S(2)}, u32[]{:S(2)}) collective-permute-start(bf16[2,1,128,640]{3,2,1,0:T(8,128)(2,1)S(1)} %get-tuple-element.119), channel_id=1, source_target_pairs={{0,1},{1,2},{2,3},{3,4},{4,5},{5,6},{6,7},{8,9},{9,10},{10,11},{11... | collective-permute-start | bytes 983048 | tf_op jit(solution)/shard_map/ppermute | solution.py:555
  6.7 15.4 %collective-permute-start.4 = (bf16[2,1,128,640]{3,2,1,0:T(8,128)(2,1)S(1)}, bf16[2,1,128,640]{3,2,1,0:T(8,128)(2,1)S(1)}, u32[]{:S(2)}, u32[]{:S(2)}) collective-permute-start(bf16[2,1,128,640]{3,2,1,0:T(8,128)(2,1)S(1)} %get-tuple-element.120), channel_id=1, source_target_pairs={{1,0},{2,1},{3,2},{4,3},{5,4},{6,5},{7,6},{9,8},{10,9},{11,10},{12... | collective-permute-start | bytes 983048 | tf_op jit(solution)/shard_map/ppermute | solution.py:556
  15.8 18.1 %collective-permute-start = (bf16[2,64,320]{2,1,0:T(8,128)(2,1)S(1)}, bf16[2,64,320]{2,1,0:T(8,128)(2,1)S(1)}, u32[]{:S(2)}, u32[]{:S(2)}) collective-permute-start(bf16[2,64,320]{2,1,0:T(8,128)(2,1)S(1)} %get-tuple-element.116), channel_id=1, source_target_pairs={{0,8},{8,16},{16,24},{24,0},{1,9},{9,17},{17,25},{25,1},{2,10},{10... | collective-permute-start | bytes 245768 | tf_op jit(solution)/shard_map/ppermute | solution.py:568
  18.2 15.7 %collective-permute-start.1 = (bf16[2,64,320]{2,1,0:T(8,128)(2,1)S(1)}, bf16[2,64,320]{2,1,0:T(8,128)(2,1)S(1)}, u32[]{:S(2)}, u32[]{:S(2)}) collective-permute-start(bf16[2,64,320]{2,1,0:T(8,128)(2,1)S(1)} %get-tuple-element.117), channel_id=1, source_target_pairs={{0,16},{8,24},{16,0},{24,8},{1,17},{9,25},{17,1},{25,9},{2,18},{10... | collective-permute-start | bytes 245768 | tf_op jit(solution)/shard_map/ppermute | solution.py:568
  20.8 10.2 %collective-permute-start.2 = (bf16[2,64,320]{2,1,0:T(8,128)(2,1)S(1)}, bf16[2,64,320]{2,1,0:T(8,128)(2,1)S(1)}, u32[]{:S(2)}, u32[]{:S(2)}) collective-permute-start(bf16[2,64,320]{2,1,0:T(8,128)(2,1)S(1)} %get-tuple-element.118), channel_id=1, source_target_pairs={{0,24},{8,0},{16,8},{24,16},{1,25},{9,1},{17,9},{25,17},{2,26},{10... | collective-permute-start | bytes 245768 | tf_op jit(solution)/shard_map/ppermute | solution.py:568
  30.7 10.6 %collective-permute-start.6 = (bf16[2,64,320]{2,1,0:T(8,128)(2,1)S(1)}, bf16[2,64,320]{2,1,0:T(8,128)(2,1)S(1)}, u32[]{:S(2)}, u32[]{:S(2)}) collective-permute-start(bf16[2,64,320]{2,1,0:T(8,128)(2,1)S(1)} %get-tuple-element.126), channel_id=1, source_target_pairs={{0,16},{8,24},{16,0},{24,8},{1,17},{9,25},{17,1},{25,9},{2,18},{10... | collective-permute-start | bytes 245768 | tf_op jit(solution)/shard_map/ppermute | solution.py:568
  31.0 10.3 %collective-permute-start.7 = (bf16[2,64,320]{2,1,0:T(8,128)(2,1)S(1)}, bf16[2,64,320]{2,1,0:T(8,128)(2,1)S(1)}, u32[]{:S(2)}, u32[]{:S(2)}) collective-permute-start(bf16[2,64,320]{2,1,0:T(8,128)(2,1)S(1)} %get-tuple-element.127), channel_id=1, source_target_pairs={{0,24},{8,0},{16,8},{24,16},{1,25},{9,1},{17,9},{25,17},{2,26},{10... | collective-permute-start | bytes 245768 | tf_op jit(solution)/shard_map/ppermute | solution.py:568
  34.6 14.6 %collective-permute-start.8 = (bf16[2,64,320]{2,1,0:T(8,128)(2,1)S(1)}, bf16[2,64,320]{2,1,0:T(8,128)(2,1)S(1)}, u32[]{:S(2)}, u32[]{:S(2)}) collective-permute-start(bf16[2,64,320]{2,1,0:T(8,128)(2,1)S(1)} %get-tuple-element.130), channel_id=1, source_target_pairs={{0,24},{8,0},{16,8},{24,16},{1,25},{9,1},{17,9},{25,17},{2,26},{10... | collective-permute-start | bytes 245768 | tf_op jit(solution)/shard_map/ppermute | solution.py:577
  35.9 16.0 %collective-permute-start.9 = (bf16[2,64,320]{2,1,0:T(8,128)(2,1)S(1)}, bf16[2,64,320]{2,1,0:T(8,128)(2,1)S(1)}, u32[]{:S(2)}, u32[]{:S(2)}) collective-permute-start(bf16[2,64,320]{2,1,0:T(8,128)(2,1)S(1)} %get-tuple-element.131), channel_id=1, source_target_pairs={{0,16},{8,24},{16,0},{24,8},{1,17},{9,25},{17,1},{25,9},{2,18},{10... | collective-permute-start | bytes 245768 | tf_op jit(solution)/shard_map/ppermute | solution.py:577
  37.1 14.8 %collective-permute-start.10 = (bf16[2,64,320]{2,1,0:T(8,128)(2,1)S(1)}, bf16[2,64,320]{2,1,0:T(8,128)(2,1)S(1)}, u32[]{:S(2)}, u32[]{:S(2)}) collective-permute-start(bf16[2,64,320]{2,1,0:T(8,128)(2,1)S(1)} %get-tuple-element.132), channel_id=1, source_target_pairs={{0,8},{8,16},{16,24},{24,0},{1,9},{9,17},{17,25},{25,1},{2,10},{10... | collective-permute-start | bytes 245768 | tf_op jit(solution)/shard_map/ppermute | solution.py:577
  42.0 16.7 %collective-permute-start.11 = (bf16[2,64,320]{2,1,0:T(8,128)(2,1)S(1)}, bf16[2,64,320]{2,1,0:T(8,128)(2,1)S(1)}, u32[]{:S(2)}, u32[]{:S(2)}) collective-permute-start(bf16[2,64,320]{2,1,0:T(8,128)(2,1)S(1)} %get-tuple-element.141), channel_id=1, source_target_pairs={{0,24},{8,0},{16,8},{24,16},{1,25},{9,1},{17,9},{25,17},{2,26},{10... | collective-permute-start | bytes 245768 | tf_op jit(solution)/shard_map/ppermute | solution.py:577
  49.2 11.1 %collective-permute-start.12 = (bf16[2,64,320]{2,1,0:T(8,128)(2,1)S(1)}, bf16[2,64,320]{2,1,0:T(8,128)(2,1)S(1)}, u32[]{:S(2)}, u32[]{:S(2)}) collective-permute-start(bf16[2,64,320]{2,1,0:T(8,128)(2,1)S(1)} %get-tuple-element.142), channel_id=1, source_target_pairs={{0,16},{8,24},{16,0},{24,8},{1,17},{9,25},{17,1},{25,9},{2,18},{10... | collective-permute-start | bytes 245768 | tf_op jit(solution)/shard_map/ppermute | solution.py:577
  49.2 11.1 %collective-permute-start.13 = (bf16[2,64,320]{2,1,0:T(8,128)(2,1)S(1)}, bf16[2,64,320]{2,1,0:T(8,128)(2,1)S(1)}, u32[]{:S(2)}, u32[]{:S(2)}) collective-permute-start(bf16[2,64,320]{2,1,0:T(8,128)(2,1)S(1)} %get-tuple-element.143), channel_id=1, source_target_pairs={{0,8},{8,16},{16,24},{24,0},{1,9},{9,17},{17,25},{25,1},{2,10},{10... | collective-permute-start | bytes 245768 | tf_op jit(solution)/shard_map/ppermute | solution.py:577
  72.7 15.1 %collective-permute-start.16 = (bf16[16,64,640]{2,1,0:T(8,128)(2,1)S(1)}, bf16[16,64,640]{2,1,0:T(8,128)(2,1)S(1)}, u32[]{:S(2)}, u32[]{:S(2)}) collective-permute-start(bf16[16,64,640]{2,1,0:T(8,128)(2,1)S(1)} %get-tuple-element.173), channel_id=1, source_target_pairs={{0,1},{1,0},{2,3},{3,2},{4,5},{5,4},{6,7},{7,6},{8,9},{9,8},{10,11... | collective-permute-start | bytes 3932168 | tf_op jit(solution)/shard_map/ppermute | solution.py:400
  78.0 14.5 %collective-permute-start.17 = (bf16[16,64,640]{2,1,0:T(8,128)(2,1)S(1)}, bf16[16,64,640]{2,1,0:T(8,128)(2,1)S(1)}, u32[]{:S(2)}, u32[]{:S(2)}) collective-permute-start(bf16[16,64,640]{2,1,0:T(8,128)(2,1)S(1)} %get-tuple-element.176), channel_id=1, source_target_pairs={{0,1},{1,0},{2,3},{3,2},{4,5},{5,4},{6,7},{7,6},{8,9},{9,8},{10,11... | collective-permute-start | bytes 3932168 | tf_op jit(solution)/shard_map/ppermute | solution.py:400
  78.2 9.0 %collective-permute-start.15 = (bf16[8,16,640]{2,1,0:T(8,128)(2,1)S(1)}, bf16[8,16,640]{2,1,0:T(8,128)(2,1)S(1)}, u32[]{:S(2)}, u32[]{:S(2)}) collective-permute-start(bf16[8,16,640]{2,1,0:T(8,128)(2,1)S(1)} %get-tuple-element.168), channel_id=1, source_target_pairs={{0,2},{1,3},{2,0},{3,1},{4,6},{5,7},{6,4},{7,5},{8,10},{9,11},{10,... | collective-permute-start | bytes 491528 | tf_op jit(solution)/shard_map/ppermute | solution.py:420
  88.7 15.1 %collective-permute-start.19 = (bf16[8,32,640]{2,1,0:T(8,128)(2,1)S(1)}, bf16[8,32,640]{2,1,0:T(8,128)(2,1)S(1)}, u32[]{:S(2)}, u32[]{:S(2)}) collective-permute-start(bf16[8,32,640]{2,1,0:T(8,128)(2,1)S(1)} %get-tuple-element.185), channel_id=1, source_target_pairs={{0,2},{1,3},{2,0},{3,1},{4,6},{5,7},{6,4},{7,5},{8,10},{9,11},{10,... | collective-permute-start | bytes 983048 | tf_op jit(solution)/shard_map/ppermute | solution.py:420
  90.5 14.0 %collective-permute-start.20 = (bf16[8,32,640]{2,1,0:T(8,128)(2,1)S(1)}, bf16[8,32,640]{2,1,0:T(8,128)(2,1)S(1)}, u32[]{:S(2)}, u32[]{:S(2)}) collective-permute-start(bf16[8,32,640]{2,1,0:T(8,128)(2,1)S(1)} %get-tuple-element.186), channel_id=1, source_target_pairs={{0,4},{1,5},{2,6},{3,7},{4,0},{5,1},{6,2},{7,3},{8,12},{9,13},{10,... | collective-permute-start | bytes 983048 | tf_op jit(solution)/shard_map/ppermute | solution.py:420
  91.5 9.7 %collective-permute-start.18 = (bf16[4,16,640]{2,1,0:T(8,128)(2,1)S(1)}, bf16[4,16,640]{2,1,0:T(8,128)(2,1)S(1)}, u32[]{:S(2)}, u32[]{:S(2)}) collective-permute-start(bf16[4,16,640]{2,1,0:T(8,128)(2,1)S(1)} %get-tuple-element.181), channel_id=1, source_target_pairs={{0,4},{1,5},{2,6},{3,7},{4,0},{5,1},{6,2},{7,3},{8,12},{9,13},{10,... | collective-permute-start | bytes 245768 | tf_op jit(solution)/shard_map/ppermute | solution.py:420
  103.8 11.8 %collective-permute-start.25 = (bf16[8,32,640]{2,1,0:T(8,128)(2,1)S(1)}, bf16[8,32,640]{2,1,0:T(8,128)(2,1)S(1)}, u32[]{:S(2)}, u32[]{:S(2)}) collective-permute-start(bf16[8,32,640]{2,1,0:T(8,128)(2,1)S(1)} %get-tuple-element.193), channel_id=1, source_target_pairs={{0,2},{1,3},{2,0},{3,1},{4,6},{5,7},{6,4},{7,5},{8,10},{9,11},{10,... | collective-permute-start | bytes 983048 | tf_op jit(solution)/shard_map/ppermute | solution.py:420
  104.5 11.2 %collective-permute-start.26 = (bf16[8,32,640]{2,1,0:T(8,128)(2,1)S(1)}, bf16[8,32,640]{2,1,0:T(8,128)(2,1)S(1)}, u32[]{:S(2)}, u32[]{:S(2)}) collective-permute-start(bf16[8,32,640]{2,1,0:T(8,128)(2,1)S(1)} %get-tuple-element.194), channel_id=1, source_target_pairs={{0,4},{1,5},{2,6},{3,7},{4,0},{5,1},{6,2},{7,3},{8,12},{9,13},{10,... | collective-permute-start | bytes 983048 | tf_op jit(solution)/shard_map/ppermute | solution.py:420
  122.5 9.1 %collective-permute-start.36 = (bf16[64,640]{1,0:T(8,128)(2,1)S(1)}, bf16[64,640]{1,0:T(8,128)(2,1)S(1)}, u32[]{:S(2)}, u32[]{:S(2)}) collective-permute-start(bf16[64,640]{1,0:T(8,128)(2,1)S(1)} %get-tuple-element.215), channel_id=1, source_target_pairs={{0,16},{8,24},{16,0},{24,8},{1,17},{9,25},{17,1},{25,9},{2,18},{10... | collective-permute-start | bytes 245768 | tf_op jit(solution)/shard_map/ppermute | solution.py:430
  123.7 7.9 %collective-permute-start.37 = (bf16[64,640]{1,0:T(8,128)(2,1)S(1)}, bf16[64,640]{1,0:T(8,128)(2,1)S(1)}, u32[]{:S(2)}, u32[]{:S(2)}) collective-permute-start(bf16[64,640]{1,0:T(8,128)(2,1)S(1)} %get-tuple-element.216), channel_id=1, source_target_pairs={{0,24},{8,0},{16,8},{24,16},{1,25},{9,1},{17,9},{25,17},{2,26},{10... | collective-permute-start | bytes 245768 | tf_op jit(solution)/shard_map/ppermute | solution.py:430
  126.7 9.2 %collective-permute-start.33 = (bf16[64,640]{1,0:T(8,128)(2,1)S(1)}, bf16[64,640]{1,0:T(8,128)(2,1)S(1)}, u32[]{:S(2)}, u32[]{:S(2)}) collective-permute-start(bf16[64,640]{1,0:T(8,128)(2,1)S(1)} %get-tuple-element.211), channel_id=1, source_target_pairs={{0,16},{8,24},{16,0},{24,8},{1,17},{9,25},{17,1},{25,9},{2,18},{10... | collective-permute-start | bytes 245768 | tf_op jit(solution)/shard_map/ppermute | solution.py:430
  (23 other events, 132.6 us)

commit v2 on v1

--- a/solution.py
+++ b/solution.py
@@ -62,29 +62,17 @@
     return mixed[m, i]
 
 
-def forward_kernel(rows, members, members_all, edged, *refs):
-    me_ref, mixed = refs[:2]
-    edges = refs[2:4] if edged else ()
-    conv_w, gain, w_in, w_down, w_head, target = refs[2 + len(edges) : 8 + len(edges)]
-    rest = refs[8 + len(edges) :]
-    normed, normal, inv, activ, slope, hidden, attract = rest[:7]
-    sends = rest[7 : 7 + members]
-    mix_s, pred = rest[7 + members :]
+def first_part(rows, mixed, edges, conv_w, gain, w_in, normed, normal, inv, activ, slope):
     mem_dev, _, lon, _ = mixed.shape
     span = len(rows) * lon
     tile = tile_of(w_in.shape[0])
-    me = me_ref[0]
 
     def conv_step(m, carry):
         for at, i in enumerate(rows):
-            start = pl.multiple_of(m * span + at * lon, lon)
-            here = pl.ds(start, lon)
+            here = pl.ds(pl.multiple_of(m * span + at * lon, lon), lon)
             sums = [None] * 3
             for a in range(3):
-                row_b = mixed_row(mixed, edges, m, i + a - 1)
-                if a == 1:
-                    mix_s[here, :] = row_b
-                row = row_b.astype(F32)
+                row = mixed_row(mixed, edges, m, i + a - 1).astype(F32)
                 for b in range(3):
                     k = 3 * a + b
                     term = conv_w[k : k + 1, :] * row
@@ -113,9 +101,22 @@
         slope[:, at] = (
             half * (1.0 + (1.0 - tanh) * (linear * (3.0 * bend - 2.0)))
         ).astype(BF16)
-    hid = (mix_s[...].astype(F32) + dot(activ[...], w_down[...])).astype(BF16)
-    hidden[...] = hid
-    pred[...] = dot(hid, w_head[...], LAST)
+
+
+def last_part(
+    rows, members_all, info_ref, mixed, activ, w_down, w_head, target, hidden, attract, sends, pred
+):
+    mem_dev, _, lon, _ = mixed.shape
+    members = len(sends)
+    span = len(rows) * lon
+    down = dot(activ[...], w_down[...])
+    for m in range(mem_dev):
+        for at, i in enumerate(rows):
+            first = m * span + at * lon
+            hidden[first : first + lon, :] = (
+                mixed[m, i].astype(F32) + down[first : first + lon, :]
+            ).astype(BF16)
+    pred[...] = dot(hidden[...], w_head[...], LAST)
     for m in range(mem_dev):
         for at, i in enumerate(rows):
             here = pl.ds(m * span + at * lon, lon)
@@ -124,37 +125,72 @@
             attract[here, :] = error * dist * (1.0 / members_all)
     points = span // members
     for k in range(members):
-        chunk = lax.rem(me + k, members)
+        chunk = lax.rem(info_ref[0] + k, members)
         for m in range(mem_dev):
             at = pl.ds(pl.multiple_of(m * span + chunk * points, points), points)
             sends[k][m] = pred[at, :].astype(BF16)
 
 
-def forward(me, mixed, edges, conv_w, gain, w_in, w_down, w_head, target, rows, members):
+def forward_kernel(rows, members_all, *refs):
+    info_ref, mixed, conv_w, gain, w_in, w_down, w_head, target = refs[:8]
+    outs, (pred,) = refs[8:-1], refs[-1:]
+    normed, normal, inv, activ, slope, hidden, attract = outs[:7]
+    first_part(rows, mixed, (), conv_w, gain, w_in, normed, normal, inv, activ, slope)
+    last_part(
+        rows, members_all, info_ref, mixed, activ, w_down, w_head, target, hidden, attract,
+        outs[7:], pred,
+    )
+
+
+def begin_kernel(rows, info_ref, mixed, above, below, *refs):
+    first_part(rows, mixed, (above, below), *refs)
+
+
+def finish_kernel(rows, members_all, *refs):
+    info_ref, mixed, activ, w_down, w_head, target, hidden, attract = refs[:8]
+    last_part(
+        rows, members_all, info_ref, mixed, activ, w_down, w_head, target, hidden, attract,
+        refs[8:-1], refs[-1],
+    )
+
+
+def forward_shapes(mixed, w_in, w_head, rows, members):
     mem_dev, _, lon, width = mixed.shape
-    out_width = w_head.shape[0]
-    units = w_in.shape[0]
+    out_width, units = w_head.shape[0], w_in.shape[0]
     total = mem_dev * len(rows) * lon
     points = len(rows) * lon // members
-    ins = [me, mixed, *edges, conv_w, gain, w_in, w_down, w_head, target]
-    outs = [
+    early = [
         ((total, width), BF16),
         ((total, width), F32),
         ((total, 128), F32),
         ((total, units), BF16),
         ((total, units), BF16),
-        ((total, width), BF16),
-        ((total, out_width), F32),
-    ] + [((mem_dev, points, out_width), BF16)] * members
-    scratch = [
-        pltpu.VMEM((total, width), BF16),
-        pltpu.VMEM((total, out_width), F32),
     ]
-    kernel = functools.partial(
-        forward_kernel, rows, members, members * mem_dev, len(edges) > 0
-    )
-    out = call(kernel, ins, outs, scratch, 9)
+    late = [((total, width), BF16), ((total, out_width), F32)]
+    late += [((mem_dev, points, out_width), BF16)] * members
+    return early, late, [pltpu.VMEM((total, out_width), F32)]
+
+
+def forward(info, mixed, conv_w, gain, w_in, w_down, w_head, target, rows, members):
+    early, late, scratch = forward_shapes(mixed, w_in, w_head, rows, members)
+    kernel = functools.partial(forward_kernel, rows, members * mixed.shape[0])
+    ins = [info, mixed, conv_w, gain, w_in, w_down, w_head, target]
+    out = call(kernel, ins, early + late, scratch, 9)
     return out[:7], out[7:]
+
+
+def begin(info, mixed, edges, conv_w, gain, w_in, w_head, rows, members):
+    early = forward_shapes(mixed, w_in, w_head, rows, members)[0]
+    kernel = functools.partial(begin_kernel, rows)
+    return call(kernel, [info, mixed, *edges, conv_w, gain, w_in], early, [], 6)
+
+
+def finish(info, mixed, activ, w_in, w_down, w_head, target, rows, members):
+    _, late, scratch = forward_shapes(mixed, w_in, w_head, rows, members)
+    kernel = functools.partial(finish_kernel, rows, members * mixed.shape[0])
+    ins = [info, mixed, activ, w_down, w_head, target]
+    out = call(kernel, ins, late, scratch, 2)
+    return out[:2], out[2:]
 
 
 def pair_kernel(*refs):
@@ -556,41 +592,54 @@
     below = lax.ppermute(first, "space", [(i + 1, i) for i in range(spaces - 1)])
     halves = [(tuple(range(1, lat_dev - 1)), ()), ((0, lat_dev - 1), (above, below))]
 
-    saved, pulled = [], []
-    for rows, edges in halves:
-        kept, sends = forward(
-            info, mixed, edges, conv_weight, gain,
-            weight_in, weight_down, head_t, target_t, rows, members,
+    def exchange(sends):
+        return [sends[0]] + [
+            lax.ppermute(sends[k], "member", ring(members, k)) for k in range(1, members)
+        ]
+
+    def give_back(pulls):
+        return [pulls[0]] + [
+            lax.ppermute(pulls[k], "member", ring(members, members - k))
+            for k in range(1, members)
+        ]
+
+    rows_a, rows_b = halves[0][0], halves[1][0]
+    kept_a, sends = forward(
+        info, mixed, conv_weight, gain, weight_in, weight_down, head_t, target_t, rows_a, members
+    )
+    pulled_a = exchange(sends)
+    kept_b = begin(
+        info, mixed, (above, below), conv_weight, gain, weight_in, head_t, rows_b, members
+    )
+    kept_b = list(kept_b)
+    pulled_a[0], kept_b[0] = after(pulled_a[0], kept_b[0])
+    pulls_a = pair_pull(pulled_a)
+    back_a = give_back(pulls_a)
+    kept_b[3], back_a[0] = after(kept_b[3], back_a[0])
+    late, sends = finish(
+        info, mixed, kept_b[3], weight_in, weight_down, head_t, target_t, rows_b, members
+    )
+    pulled_b = exchange(sends)
+    saved = [list(kept_a), kept_b + list(late)]
+    attract_a, late_hidden = after(saved[0][6], saved[1][5])
+    saved[1][5] = late_hidden
+    grads = [
+        slopes(
+            info, attract_a, back_a, head_t, weight_down, saved[0][4], scale, share
         )
-        saved.append(kept)
-        pulled.append(
-            [sends[0]]
-            + [lax.ppermute(sends[k], "member", ring(members, k)) for k in range(1, members)]
-        )
-    pulled[0][-1], pulled[1][0] = lax.optimization_barrier((pulled[0][-1], pulled[1][0]))
-    backs = []
-    for half in range(2):
-        pulls = pair_pull(pulled[half])
-        backs.append(
-            [pulls[0]]
-            + [
-                lax.ppermute(pulls[k], "member", ring(members, members - k))
-                for k in range(1, members)
-            ]
-        )
-    backs[0][0], backs[1][0] = lax.optimization_barrier((backs[0][0], backs[1][0]))
-    grads, smalls = [], []
-    for half, (rows, edges) in enumerate(halves):
-        _, normal, inv, _, slope, _, attract = saved[half]
-        if half:
-            attract, smalls[0] = lax.optimization_barrier((attract, smalls[0]))
-        grads.append(
-            slopes(info, attract, backs[half], head_t, weight_down, slope, scale, share)
-        )
-        if half == 0:
-            smalls.append(
-                norms(grads[0][2], weight_in, normal, inv, gain, mixed, edges, rows)
-            )
+    ]
+    pulled_b[0], ghid = after(pulled_b[0], grads[0][1])
+    grads[0] = [grads[0][0], ghid, grads[0][2]]
+    pulls_b = list(pair_pull(pulled_b))
+    back_b = give_back(pulls_b)
+    gpre_a, back_b[0] = after(grads[0][2], back_b[0])
+    smalls = [
+        norms(gpre_a, weight_in, saved[0][1], saved[0][2], gain, mixed, (), rows_a)
+    ]
+    attract_b, smalls[0] = after(saved[1][6], smalls[0])
+    grads.append(
+        slopes(info, attract_b, back_b, head_t, weight_down, saved[1][4], scale, share)
+    )
 
     hids = [saved[h][5] for h in range(2)]
     depths = spaces.bit_length() - 2
@@ -643,6 +692,7 @@
     whole = spread_step(whole, 1)
     units = weight_in.shape[0] // devices
     head_total, conv_total, gain_total = placed(info, whole, out_width)
+    own_i, head_total = after(own_i, head_total)
     in_mine = add_up(own_i, others_i)[:units]
     down_mine = add_up(own_d, others_d)[:units]
     return (in_mine, down_mine, head_total.T, gain_total.reshape(width), conv_total)

time: 139 us -> 150 us (1.079)
  waiting for transfers between devices: 29 us -> 44.3 us
  starting transfers between devices: 54.9 us -> 48.8 us
  Pallas kernels: 49.4 us -> 50.9 us
    ppermute x10, starting transfers between devices: 14.2 us -> 10.3 us  [merge_blocks(): lax.ppermute(part, 'space', flip(spaces, 1 << order[depth]))]
    ppermute x6, waiting for transfers between devices: 4.61 us -> 8.41 us  [turn_blocks(): lax.ppermute(parts[k], 'member', ring(members, k))]
    ppermute x12, waiting for transfers between devices: 6.08 us -> 9.86 us  [the longest x6 9.85 us: give_back(): lax.ppermute(pulls[k], 'member', ring(members, members - k))]
    ppermute x3, waiting for transfers between devices: 2.59 us -> 6.12 us  [spread_step(): other = lax.ppermute(whole, 'space', flip(lax.axis_size('space'), bit))]
    ppermute x10, waiting for transfers between devices: 13.2 us -> 15.8 us  [merge_blocks(): lax.ppermute(part, 'space', flip(spaces, 1 << order[depth]))]
    ppermute x12, starting transfers between devices: 22.4 us -> 20 us  [the longest x6 11.7 us: exchange(): lax.ppermute(sends[k], 'member', ring(members, k))]
    ppermute x3, starting transfers between devices: 2.07 us -> 3.7 us  [fold_members(): lax.ppermute(own, 'member', ring(members, k))]
    ppermute x3, waiting for transfers between devices: 2.54 us -> 4.07 us  [fold_members(): lax.ppermute(own, 'member', ring(members, k))]
  transfers between devices with their start and end apart: 39 -> 39, of which waited for: 13 -> 16; matrix products, arithmetic and copies ran while one was open for 1% -> 1% of each run, Pallas kernels for 28% -> 26%
where the time goes in v2:
time: 150 us
  Pallas kernels  50.9 us (34%)
  starting transfers between devices  48.8 us (33%)
  waiting for transfers between devices  44.3 us (30%)
  local copies, waits for them, and re-layouts  2.44 us (2%)
  other arithmetic  2.22 us (1%)
    pallas_call x24, Pallas kernels, call(): pl.pallas_call(kernel, in_specs=[SMEM] * scalars + [pl.BlockSpec(memory_s...  50.9 us
    ppermute x10, waiting for transfers between devices, merge_blocks(): lax.ppermute(part, 'space', flip(spaces, 1 << order[depth]))  15.8 us
    ppermute x6, starting transfers between devices, exchange(): lax.ppermute(sends[k], 'member', ring(members, k))  11.7 us
    ppermute x10, starting transfers between devices, merge_blocks(): lax.ppermute(part, 'space', flip(spaces, 1 << order[depth]))  10.3 us
    ppermute x6, waiting for transfers between devices, give_back(): lax.ppermute(pulls[k], 'member', ring(members, members - k))  9.85 us
    ppermute x6, starting transfers between devices, turn_blocks(): lax.ppermute(parts[k], 'member', ring(members, k))  8.63 us
    ppermute x6, waiting for transfers between devices, turn_blocks(): lax.ppermute(parts[k], 'member', ring(members, k))  8.41 us
    ppermute x6, starting transfers between devices, give_back(): lax.ppermute(pulls[k], 'member', ring(members, members - k))  8.31 us
  transfers between devices with their start and end apart: 39, of which 16 were waited for; matrix products, arithmetic and copies ran while one was open for 1% of the time, Pallas kernels for 26%

profile of v2, /device:TPU:0, one launch (start us, length us, event | category | flops | bytes accessed | tf_op | source)
XLA Modules:
  0.0 149.6 jit_solution(16237652190677497633)
XLA Ops:
  4.0 2.7 %collective-permute-start = (bf16[2,1,128,640]{3,2,1,0:T(8,128)(2,1)S(1)}, bf16[2,1,128,640]{3,2,1,0:T(8,128)(2,1)S(1)}, u32[]{:S(2)}, u32[]{:S(2)}) collective-permute-start(bf16[2,1,128,640]{3,2,1,0:T(8,128)(2,1)S(1)} %get-tuple-element.123), channel_id=1, source_target_pairs={{0,1},{1,2},{2,3},{3,4},{4,5},{5,6},{6,7},{8,9},{9,10},{10,11},{11... | collective-permute-start | bytes 983048 | tf_op jit(solution)/shard_map/ppermute | solution.py:591
  8.1 7.8 %shard_map.120 = (bf16[512,640]{1,0:T(8,128)(2,1)S(1)}, f32[512,640]{1,0:T(8,128)S(1)}, f32[512,128]{1,0:T(8,128)S(1)}, bf16[512,1920]{1,0:T(8,128)(2,1)S(1)}, b...) custom-call(s32[4]{0:T(128)S(1)} %pad_add_fusion.info_ref.refs_0_, ...), custom_call_target="tpu_custom_call" | custom-call | flops 8999999488 | bytes 15115280 | tf_op jit(solution)/shard_map/pallas_call | solution.py:39
  18.4 2.6 %collective-permute-start.3 = (bf16[2,64,320]{2,1,0:T(8,128)(2,1)S(1)}, bf16[2,64,320]{2,1,0:T(8,128)(2,1)S(1)}, u32[]{:S(2)}, u32[]{:S(2)}) collective-permute-start(bf16[2,64,320]{2,1,0:T(8,128)(2,1)S(1)} %get-tuple-element.130), channel_id=1, source_target_pairs={{0,16},{8,24},{16,0},{24,8},{1,17},{9,25},{17,1},{25,9},{2,18},{10... | collective-permute-start | bytes 245768 | tf_op jit(solution)/shard_map/ppermute | solution.py:597
  22.3 5.2 %shard_map.121 = (bf16[512,640]{1,0:T(8,128)(2,1)S(1)}, f32[512,640]{1,0:T(8,128)S(1)}, f32[512,128]{1,0:T(8,128)S(1)}, bf16[512,1920]{1,0:T(8,128)(2,1)S(1)}, bf16[512,1920]{1,0:T(8,128)(2,1)S(1)}) custom-call(s32[4]{0:T(128)S(1)} %pad_add_fusion.info_ref.refs_0_, bf16[2,4,128,640]{3,2,1,0:T(8,128)(2,1)S(1)} %get-tuple-element.121.refs_1_.mixed.refs_5_, ...), custom_call_target="tpu_custom_call" | custom-call | flops 6000000000 | bytes 10609680 | tf_op jit(solution)/shard_map/pallas_call | solution.py:39
  28.3 3.5 %collective-permute-start.5 = (bf16[2,64,320]{2,1,0:T(8,128)(2,1)S(1)}, bf16[2,64,320]{2,1,0:T(8,128)(2,1)S(1)}, u32[]{:S(2)}, u32[]{:S(2)}) collective-permute-start(bf16[2,64,320]{2,1,0:T(8,128)(2,1)S(1)} %get-tuple-element.137), channel_id=1, source_target_pairs={{0,24},{8,0},{16,8},{24,16},{1,25},{9,1},{17,9},{25,17},{2,26},{10... | collective-permute-start | bytes 245768 | tf_op jit(solution)/shard_map/ppermute | solution.py:602
  32.5 3.4 %shard_map.123 = (bf16[512,640]{1,0:T(8,128)(2,1)S(1)}, f32[512,320]{1,0:T(8,128)S(1)}, bf16[2,64,320]{2,1,0:T(8,128)(2,1)S(1)}, bf16[2,64,320]{2,1,0:T(8,128)(2...) custom-call(s32[4]{0:T(128)S(1)} %pad_add_fusion.info_ref.refs_0_, ...), custom_call_target="tpu_custom_call" | custom-call | flops 2000000000 | bytes 8437776 | tf_op jit(solution)/shard_map/pallas_call | solution.py:39
  35.9 2.8 %collective-permute-start.8 = (bf16[2,64,320]{2,1,0:T(8,128)(2,1)S(1)}, bf16[2,64,320]{2,1,0:T(8,128)(2,1)S(1)}, u32[]{:S(2)}, u32[]{:S(2)}) collective-permute-start(bf16[2,64,320]{2,1,0:T(8,128)(2,1)S(1)} %get-tuple-element.147), channel_id=1, source_target_pairs={{0,8},{8,16},{16,24},{24,0},{1,9},{9,17},{17,25},{25,1},{2,10},{10... | collective-permute-start | bytes 245768 | tf_op jit(solution)/shard_map/ppermute | solution.py:597
  41.2 5.3 %collective-permute-done.6.refs_4_ = bf16[2,64,320]{2,1,0:T(8,128)(2,1)S(1)} collective-permute-done((bf16[2,64,320]{2,1,0:T(8,128)(2,1)S(1)}, bf16[2,64,320]{2,1,0:T(8,128)(2,1)S(1)}, u32[]{:S(2)}, u32[]{:S(2)}) %collective-permute-start.6) | collective-permute-done | bytes 81952 | tf_op jit(solution)/shard_map/ppermute | solution.py:602
  46.4 3.0 %shard_map.124 = (bf16[512,320]{1,0:T(8,128)(2,1)S(1)}, bf16[512,640]{1,0:T(8,128)(2,1)S(1)}, bf16[512,1920]{1,0:T(8,128)(2,1)S(1)}) custom-call(s32[4]{0:T(128)S(1)} %pad_add_fusion.info_ref.refs_0_, f32[512,320]{1,0:T(8,128)S(1)} %get-tuple-element.135.refs_1_, bf16[2,64,320]{2,1,0:T(8,128)(2,1)S(1)} %get-tuple-element.136.refs_2_, ...), custom_call_target="tpu_custom_call" | custom-call | flops 3000000000 | bytes 8765456 | tf_op jit(solution)/shard_map/pallas_call | solution.py:39
  50.2 3.5 %collective-permute-start.11 = (bf16[2,64,320]{2,1,0:T(8,128)(2,1)S(1)}, bf16[2,64,320]{2,1,0:T(8,128)(2,1)S(1)}, u32[]{:S(2)}, u32[]{:S(2)}) collective-permute-start(bf16[2,64,320]{2,1,0:T(8,128)(2,1)S(1)} %get-tuple-element.156), channel_id=1, source_target_pairs={{0,24},{8,0},{16,8},{24,16},{1,25},{9,1},{17,9},{25,17},{2,26},{10... | collective-permute-start | bytes 245768 | tf_op jit(solution)/shard_map/ppermute | solution.py:602
  54.3 4.0 %shard_map.126.refs_4_ = f32[16,640]{1,0:T(8,128)S(1)} custom-call(bf16[512,1920]{1,0:T(8,128)(2,1)S(1)} %get-tuple-element.151.refs_0_.left_a, bf16[1920,640]{1,0:T(8,128)(2,1)S(1)} %copy-done.1, f32[512,640]{1,0:T(8,128)S(1)} %get-tuple-element.152.refs_2_, f32[512,128]{1,0:T(8,128)S(1)} %get-tuple-element.153.refs_3_, ...), custom_call_target="tpu_custom_call" | custom-call | flops 5000000000 | bytes 7350784 | tf_op jit(solution)/shard_map/pallas_call | solution.py:39
  58.4 4.6 %collective-permute-done.12.refs_4_ = bf16[2,64,320]{2,1,0:T(8,128)(2,1)S(1)} collective-permute-done((bf16[2,64,320]{2,1,0:T(8,128)(2,1)S(1)}, bf16[2,64,320]{2,1,0:T(8,128)(2,1)S(1)}, u32[]{:S(2)}, u32[]{:S(2)}) %collective-permute-start.12) | collective-permute-done | bytes 81952 | tf_op jit(solution)/shard_map/ppermute | solution.py:602
  62.9 3.0 %shard_map.127 = (bf16[512,320]{1,0:T(8,128)(2,1)S(1)}, bf16[512,640]{1,0:T(8,128)(2,1)S(1)}, bf16[512,1920]{1,0:T(8,128)(2,1)S(1)}) custom-call(s32[4]{0:T(128)S(1)} %pad_add_fusion.info_ref.refs_0_, f32[512,320]{1,0:T(8,128)S(1)} %get-tuple-element.154.refs_1_, bf16[2,64,320]{2,1,0:T(8,128)(2,1)S(1)} %get-tuple-element.155.refs_2_, ...), custom_call_target="tpu_custom_call" | custom-call | flops 3000000000 | bytes 8765456 | tf_op jit(solution)/shard_map/pallas_call | solution.py:39
  65.9 4.0 %shard_map.128.refs_5_ = f32[16,640]{1,0:T(8,128)S(1)} custom-call(bf16[512,1920]{1,0:T(8,128)(2,1)S(1)} %get-tuple-element.177.refs_0_.left_b, bf16[1920,640]{1,0:T(8,128)(2,1)S(1)} %copy-done.1, f32[512,640]{1,0:T(8,128)S(1)} %get-tuple-element.165.refs_2_, f32[512,128]{1,0:T(8,128)S(1)} %get-tuple-element.166.refs_3_, ...), custom_call_target="tpu_custom_call" | custom-call | flops 5000000000 | bytes 8006144 | tf_op jit(solution)/shard_map/pallas_call | solution.py:39
  71.4 4.0 %shard_map.130 = (f32[16,64,640]{2,1,0:T(8,128)S(1)}, bf16[16,64,640]{2,1,0:T(8,128)(2,1)S(1)}) custom-call(s32[4]{0:T(128)S(1)} %pad_add_fusion.info_ref.refs_0_, bf16[512,1920]{1,0:T(8,128)(2,1)S(1)} %get-tuple-element.168.left_a, bf16[512,1920]{1,0:T(8,128)(2,1)S(1)} %get-tuple-element.133.refs_2_.left_b, ...), custom_call_target="tpu_custom_call" | custom-call | flops 6000000000 | bytes 9175056 | tf_op jit(solution)/shard_map/pallas_call | solution.py:39
  76.9 4.0 %shard_map.132 = (f32[16,64,640]{2,1,0:T(8,128)S(1)}, bf16[16,64,640]{2,1,0:T(8,128)(2,1)S(1)}) custom-call(s32[4]{0:T(128)S(1)} %pad_add_fusion.info_ref.refs_0_, bf16[512,1920]{1,0:T(8,128)(2,1)S(1)} %get-tuple-element.151.refs_0_.left_a, bf16[512,1920]{1,0:T(8,128)(2,1)S(1)} %get-tuple-element.177.refs_0_.left_b, ...), custom_call_target="tpu_custom_call" | custom-call | flops 6000000000 | bytes 9175056 | tf_op jit(solution)/shard_map/pallas_call | solution.py:39
  83.1 4.8 %collective-permute-done.15.refs_1_ = bf16[8,16,640]{2,1,0:T(8,128)(2,1)S(1)} collective-permute-done((bf16[8,16,640]{2,1,0:T(8,128)(2,1)S(1)}, bf16[8,16,640]{2,1,0:T(8,128)(2,1)S(1)}, u32[]{:S(2)}, u32[]{:S(2)}) %collective-permute-start.15) | collective-permute-done | bytes 163872 | tf_op jit(solution)/shard_map/ppermute | solution.py:456
  94.1 7.7 %collective-permute-done.18.got = bf16[4,16,640]{2,1,0:T(8,128)(2,1)S(1)} collective-permute-done((bf16[4,16,640]{2,1,0:T(8,128)(2,1)S(1)}, bf16[4,16,640]{2,1,0:T(8,128)(2,1)S(1)}, u32[]{:S(2)}, u32[]{:S(2)}) %collective-permute-start.18) | collective-permute-done | bytes 81952 | tf_op jit(solution)/shard_map/ppermute | solution.py:456
  108.2 3.5 %collective-permute-done.22.refs_2_ = bf16[4,16,640]{2,1,0:T(8,128)(2,1)S(1)} collective-permute-done((bf16[4,16,640]{2,1,0:T(8,128)(2,1)S(1)}, bf16[4,16,640]{2,1,0:T(8,128)(2,1)S(1)}, u32[]{:S(2)}, u32[]{:S(2)}) %collective-permute-start.22) | collective-permute-done | bytes 81952 | tf_op jit(solution)/shard_map/ppermute | solution.py:519
  114.8 2.6 %collective-permute-done.24 = bf16[1,4,16,640]{3,2,1,0:T(8,128)(2,1)S(1)} collective-permute-done((bf16[1,4,16,640]{3,2,1,0:T(8,128)(2,1)S(1)}, bf16[1,4,16,640]{3,2,1,0:T(8,128)(2,1)S(1)}, u32[]{:S(2)}, u32[]{:S(2)}) %collective-permute-start.24) | collective-permute-done | bytes 81952 | tf_op jit(solution)/shard_map/ppermute | solution.py:528
  122.8 3.5 %collective-permute-done.29 = bf16[2,4,16,640]{3,2,1,0:T(8,128)(2,1)S(1)} collective-permute-done((bf16[2,4,16,640]{3,2,1,0:T(8,128)(2,1)S(1)}, bf16[2,4,16,640]{3,2,1,0:T(8,128)(2,1)S(1)}, u32[]{:S(2)}, u32[]{:S(2)}) %collective-permute-start.29) | collective-permute-done | bytes 163872 | tf_op jit(solution)/shard_map/ppermute | solution.py:528
  130.4 2.8 %collective-permute-start.38 = (bf16[64,640]{1,0:T(8,128)(2,1)S(1)}, bf16[64,640]{1,0:T(8,128)(2,1)S(1)}, u32[]{:S(2)}, u32[]{:S(2)}) collective-permute-start(bf16[64,640]{1,0:T(8,128)(2,1)S(1)} %get-tuple-element.233), channel_id=1, source_target_pairs={{0,24},{8,0},{16,8},{24,16},{1,25},{9,1},{17,9},{25,17},{2,26},{10... | collective-permute-start | bytes 245768 | tf_op jit(solution)/shard_map/ppermute | solution.py:466
  133.3 2.9 %collective-permute-done.36 = bf16[64,640]{1,0:T(8,128)(2,1)S(1)} collective-permute-done((bf16[64,640]{1,0:T(8,128)(2,1)S(1)}, bf16[64,640]{1,0:T(8,128)(2,1)S(1)}, u32[]{:S(2)}, u32[]{:S(2)}) %collective-permute-start.36) | collective-permute-done | bytes 81952 | tf_op jit(solution)/shard_map/ppermute | solution.py:466
  136.1 3.0 %collective-permute-done.37 = bf16[64,640]{1,0:T(8,128)(2,1)S(1)} collective-permute-done((bf16[64,640]{1,0:T(8,128)(2,1)S(1)}, bf16[64,640]{1,0:T(8,128)(2,1)S(1)}, u32[]{:S(2)}, u32[]{:S(2)}) %collective-permute-start.37) | collective-permute-done | bytes 81952 | tf_op jit(solution)/shard_map/ppermute | solution.py:466
  (102 shorter events, 54.5 us)
Async XLA Ops:
  4.0 18.3 %collective-permute-start = (bf16[2,1,128,640]{3,2,1,0:T(8,128)(2,1)S(1)}, bf16[2,1,128,640]{3,2,1,0:T(8,128)(2,1)S(1)}, u32[]{:S(2)}, u32[]{:S(2)}) collective-permute-start(bf16[2,1,128,640]{3,2,1,0:T(8,128)(2,1)S(1)} %get-tuple-element.123), channel_id=1, source_target_pairs={{0,1},{1,2},{2,3},{3,4},{4,5},{5,6},{6,7},{8,9},{9,10},{10,11},{11... | collective-permute-start | bytes 983048 | tf_op jit(solution)/shard_map/ppermute | solution.py:591
  6.7 15.6 %collective-permute-start.1 = (bf16[2,1,128,640]{3,2,1,0:T(8,128)(2,1)S(1)}, bf16[2,1,128,640]{3,2,1,0:T(8,128)(2,1)S(1)}, u32[]{:S(2)}, u32[]{:S(2)}) collective-permute-start(bf16[2,1,128,640]{3,2,1,0:T(8,128)(2,1)S(1)} %get-tuple-element.124), channel_id=1, source_target_pairs={{1,0},{2,1},{3,2},{4,3},{5,4},{6,5},{7,6},{9,8},{10,9},{11,10},{12... | collective-permute-start | bytes 983048 | tf_op jit(solution)/shard_map/ppermute | solution.py:592
  15.9 11.6 %collective-permute-start.2 = (bf16[2,64,320]{2,1,0:T(8,128)(2,1)S(1)}, bf16[2,64,320]{2,1,0:T(8,128)(2,1)S(1)}, u32[]{:S(2)}, u32[]{:S(2)}) collective-permute-start(bf16[2,64,320]{2,1,0:T(8,128)(2,1)S(1)} %get-tuple-element.129), channel_id=1, source_target_pairs={{0,8},{8,16},{16,24},{24,0},{1,9},{9,17},{17,25},{25,1},{2,10},{10... | collective-permute-start | bytes 245768 | tf_op jit(solution)/shard_map/ppermute | solution.py:597
  18.4 9.2 %collective-permute-start.3 = (bf16[2,64,320]{2,1,0:T(8,128)(2,1)S(1)}, bf16[2,64,320]{2,1,0:T(8,128)(2,1)S(1)}, u32[]{:S(2)}, u32[]{:S(2)}) collective-permute-start(bf16[2,64,320]{2,1,0:T(8,128)(2,1)S(1)} %get-tuple-element.130), channel_id=1, source_target_pairs={{0,16},{8,24},{16,0},{24,8},{1,17},{9,25},{17,1},{25,9},{2,18},{10... | collective-permute-start | bytes 245768 | tf_op jit(solution)/shard_map/ppermute | solution.py:597
  28.3 12.0 %collective-permute-start.5 = (bf16[2,64,320]{2,1,0:T(8,128)(2,1)S(1)}, bf16[2,64,320]{2,1,0:T(8,128)(2,1)S(1)}, u32[]{:S(2)}, u32[]{:S(2)}) collective-permute-start(bf16[2,64,320]{2,1,0:T(8,128)(2,1)S(1)} %get-tuple-element.137), channel_id=1, source_target_pairs={{0,24},{8,0},{16,8},{24,16},{1,25},{9,1},{17,9},{25,17},{2,26},{10... | collective-permute-start | bytes 245768 | tf_op jit(solution)/shard_map/ppermute | solution.py:602
  31.7 14.7 %collective-permute-start.6 = (bf16[2,64,320]{2,1,0:T(8,128)(2,1)S(1)}, bf16[2,64,320]{2,1,0:T(8,128)(2,1)S(1)}, u32[]{:S(2)}, u32[]{:S(2)}) collective-permute-start(bf16[2,64,320]{2,1,0:T(8,128)(2,1)S(1)} %get-tuple-element.138), channel_id=1, source_target_pairs={{0,16},{8,24},{16,0},{24,8},{1,17},{9,25},{17,1},{25,9},{2,18},{10... | collective-permute-start | bytes 245768 | tf_op jit(solution)/shard_map/ppermute | solution.py:602
  32.5 14.0 %collective-permute-start.7 = (bf16[2,64,320]{2,1,0:T(8,128)(2,1)S(1)}, bf16[2,64,320]{2,1,0:T(8,128)(2,1)S(1)}, u32[]{:S(2)}, u32[]{:S(2)}) collective-permute-start(bf16[2,64,320]{2,1,0:T(8,128)(2,1)S(1)} %get-tuple-element.139), channel_id=1, source_target_pairs={{0,8},{8,16},{16,24},{24,0},{1,9},{9,17},{17,25},{25,1},{2,10},{10... | collective-permute-start | bytes 245768 | tf_op jit(solution)/shard_map/ppermute | solution.py:602
  35.9 13.5 %collective-permute-start.8 = (bf16[2,64,320]{2,1,0:T(8,128)(2,1)S(1)}, bf16[2,64,320]{2,1,0:T(8,128)(2,1)S(1)}, u32[]{:S(2)}, u32[]{:S(2)}) collective-permute-start(bf16[2,64,320]{2,1,0:T(8,128)(2,1)S(1)} %get-tuple-element.147), channel_id=1, source_target_pairs={{0,8},{8,16},{16,24},{24,0},{1,9},{9,17},{17,25},{25,1},{2,10},{10... | collective-permute-start | bytes 245768 | tf_op jit(solution)/shard_map/ppermute | solution.py:597
  38.7 10.7 %collective-permute-start.9 = (bf16[2,64,320]{2,1,0:T(8,128)(2,1)S(1)}, bf16[2,64,320]{2,1,0:T(8,128)(2,1)S(1)}, u32[]{:S(2)}, u32[]{:S(2)}) collective-permute-start(bf16[2,64,320]{2,1,0:T(8,128)(2,1)S(1)} %get-tuple-element.148), channel_id=1, source_target_pairs={{0,16},{8,24},{16,0},{24,8},{1,17},{9,25},{17,1},{25,9},{2,18},{10... | collective-permute-start | bytes 245768 | tf_op jit(solution)/shard_map/ppermute | solution.py:597
  40.3 9.1 %collective-permute-start.10 = (bf16[2,64,320]{2,1,0:T(8,128)(2,1)S(1)}, bf16[2,64,320]{2,1,0:T(8,128)(2,1)S(1)}, u32[]{:S(2)}, u32[]{:S(2)}) collective-permute-start(bf16[2,64,320]{2,1,0:T(8,128)(2,1)S(1)} %get-tuple-element.149), channel_id=1, source_target_pairs={{0,24},{8,0},{16,8},{24,16},{1,25},{9,1},{17,9},{25,17},{2,26},{10... | collective-permute-start | bytes 245768 | tf_op jit(solution)/shard_map/ppermute | solution.py:597
  50.2 8.2 %collective-permute-start.11 = (bf16[2,64,320]{2,1,0:T(8,128)(2,1)S(1)}, bf16[2,64,320]{2,1,0:T(8,128)(2,1)S(1)}, u32[]{:S(2)}, u32[]{:S(2)}) collective-permute-start(bf16[2,64,320]{2,1,0:T(8,128)(2,1)S(1)} %get-tuple-element.156), channel_id=1, source_target_pairs={{0,24},{8,0},{16,8},{24,16},{1,25},{9,1},{17,9},{25,17},{2,26},{10... | collective-permute-start | bytes 245768 | tf_op jit(solution)/shard_map/ppermute | solution.py:602
  53.7 9.2 %collective-permute-start.12 = (bf16[2,64,320]{2,1,0:T(8,128)(2,1)S(1)}, bf16[2,64,320]{2,1,0:T(8,128)(2,1)S(1)}, u32[]{:S(2)}, u32[]{:S(2)}) collective-permute-start(bf16[2,64,320]{2,1,0:T(8,128)(2,1)S(1)} %get-tuple-element.157), channel_id=1, source_target_pairs={{0,16},{8,24},{16,0},{24,8},{1,17},{9,25},{17,1},{25,9},{2,18},{10... | collective-permute-start | bytes 245768 | tf_op jit(solution)/shard_map/ppermute | solution.py:602
  53.7 9.2 %collective-permute-start.13 = (bf16[2,64,320]{2,1,0:T(8,128)(2,1)S(1)}, bf16[2,64,320]{2,1,0:T(8,128)(2,1)S(1)}, u32[]{:S(2)}, u32[]{:S(2)}) collective-permute-start(bf16[2,64,320]{2,1,0:T(8,128)(2,1)S(1)} %get-tuple-element.158), channel_id=1, source_target_pairs={{0,8},{8,16},{16,24},{24,0},{1,9},{9,17},{17,25},{25,1},{2,10},{10... | collective-permute-start | bytes 245768 | tf_op jit(solution)/shard_map/ppermute | solution.py:602
  75.5 13.1 %collective-permute-start.16 = (bf16[16,64,640]{2,1,0:T(8,128)(2,1)S(1)}, bf16[16,64,640]{2,1,0:T(8,128)(2,1)S(1)}, u32[]{:S(2)}, u32[]{:S(2)}) collective-permute-start(bf16[16,64,640]{2,1,0:T(8,128)(2,1)S(1)} %get-tuple-element.187), channel_id=1, source_target_pairs={{0,1},{1,0},{2,3},{3,2},{4,5},{5,4},{6,7},{7,6},{8,9},{9,8},{10,11... | collective-permute-start | bytes 3932168 | tf_op jit(solution)/shard_map/ppermute | solution.py:436
  80.9 12.3 %collective-permute-start.17 = (bf16[16,64,640]{2,1,0:T(8,128)(2,1)S(1)}, bf16[16,64,640]{2,1,0:T(8,128)(2,1)S(1)}, u32[]{:S(2)}, u32[]{:S(2)}) collective-permute-start(bf16[16,64,640]{2,1,0:T(8,128)(2,1)S(1)} %get-tuple-element.190), channel_id=1, source_target_pairs={{0,1},{1,0},{2,3},{3,2},{4,5},{5,4},{6,7},{7,6},{8,9},{9,8},{10,11... | collective-permute-start | bytes 3932168 | tf_op jit(solution)/shard_map/ppermute | solution.py:436
  89.4 16.7 %collective-permute-start.19 = (bf16[8,32,640]{2,1,0:T(8,128)(2,1)S(1)}, bf16[8,32,640]{2,1,0:T(8,128)(2,1)S(1)}, u32[]{:S(2)}, u32[]{:S(2)}) collective-permute-start(bf16[8,32,640]{2,1,0:T(8,128)(2,1)S(1)} %get-tuple-element.199), channel_id=1, source_target_pairs={{0,2},{1,3},{2,0},{3,1},{4,6},{5,7},{6,4},{7,5},{8,10},{9,11},{10,... | collective-permute-start | bytes 983048 | tf_op jit(solution)/shard_map/ppermute | solution.py:456
  91.2 15.3 %collective-permute-start.20 = (bf16[8,32,640]{2,1,0:T(8,128)(2,1)S(1)}, bf16[8,32,640]{2,1,0:T(8,128)(2,1)S(1)}, u32[]{:S(2)}, u32[]{:S(2)}) collective-permute-start(bf16[8,32,640]{2,1,0:T(8,128)(2,1)S(1)} %get-tuple-element.200), channel_id=1, source_target_pairs={{0,4},{1,5},{2,6},{3,7},{4,0},{5,1},{6,2},{7,3},{8,12},{9,13},{10,... | collective-permute-start | bytes 983048 | tf_op jit(solution)/shard_map/ppermute | solution.py:456
  91.2 10.7 %collective-permute-start.18 = (bf16[4,16,640]{2,1,0:T(8,128)(2,1)S(1)}, bf16[4,16,640]{2,1,0:T(8,128)(2,1)S(1)}, u32[]{:S(2)}, u32[]{:S(2)}) collective-permute-start(bf16[4,16,640]{2,1,0:T(8,128)(2,1)S(1)} %get-tuple-element.195), channel_id=1, source_target_pairs={{0,4},{1,5},{2,6},{3,7},{4,0},{5,1},{6,2},{7,3},{8,12},{9,13},{10,... | collective-permute-start | bytes 245768 | tf_op jit(solution)/shard_map/ppermute | solution.py:456
  103.8 7.8 %collective-permute-start.22 = (bf16[4,16,640]{2,1,0:T(8,128)(2,1)S(1)}, bf16[4,16,640]{2,1,0:T(8,128)(2,1)S(1)}, u32[]{:S(2)}, u32[]{:S(2)}) collective-permute-start(bf16[4,16,640]{2,1,0:T(8,128)(2,1)S(1)} %shard_map.136.refs_0_), channel_id=1, source_target_pairs={{0,16},{8,24},{16,0},{24,8},{1,17},{9,25},{17,1},{25,9},{2,18},{10... | collective-permute-start | bytes 245768 | tf_op jit(solution)/shard_map/ppermute | solution.py:519
  106.1 11.2 %collective-permute-start.25 = (bf16[8,32,640]{2,1,0:T(8,128)(2,1)S(1)}, bf16[8,32,640]{2,1,0:T(8,128)(2,1)S(1)}, u32[]{:S(2)}, u32[]{:S(2)}) collective-permute-start(bf16[8,32,640]{2,1,0:T(8,128)(2,1)S(1)} %get-tuple-element.207), channel_id=1, source_target_pairs={{0,2},{1,3},{2,0},{3,1},{4,6},{5,7},{6,4},{7,5},{8,10},{9,11},{10,... | collective-permute-start | bytes 983048 | tf_op jit(solution)/shard_map/ppermute | solution.py:456
  106.5 10.9 %collective-permute-start.26 = (bf16[8,32,640]{2,1,0:T(8,128)(2,1)S(1)}, bf16[8,32,640]{2,1,0:T(8,128)(2,1)S(1)}, u32[]{:S(2)}, u32[]{:S(2)}) collective-permute-start(bf16[8,32,640]{2,1,0:T(8,128)(2,1)S(1)} %get-tuple-element.208), channel_id=1, source_target_pairs={{0,4},{1,5},{2,6},{3,7},{4,0},{5,1},{6,2},{7,3},{8,12},{9,13},{10,... | collective-permute-start | bytes 983048 | tf_op jit(solution)/shard_map/ppermute | solution.py:456
  128.8 15.3 %collective-permute-start.32 = (bf16[4,4,16,640]{3,2,1,0:T(8,128)(2,1)S(1)}, bf16[4,4,16,640]{3,2,1,0:T(8,128)(2,1)S(1)}, u32[]{:S(2)}, u32[]{:S(2)}) collective-permute-start(bf16[4,4,16,640]{3,2,1,0:T(8,128)(2,1)S(1)} %pad_maximum_fusion.1), channel_id=1, source_target_pairs={{0,1},{1,0},{2,3},{3,2},{4,5},{5,4},{6,7},{7,6},{8,9},{9,8},{10,11... | collective-permute-start | bytes 983048 | tf_op jit(solution)/shard_map/ppermute | solution.py:528
  129.7 9.4 %collective-permute-start.37 = (bf16[64,640]{1,0:T(8,128)(2,1)S(1)}, bf16[64,640]{1,0:T(8,128)(2,1)S(1)}, u32[]{:S(2)}, u32[]{:S(2)}) collective-permute-start(bf16[64,640]{1,0:T(8,128)(2,1)S(1)} %get-tuple-element.232), channel_id=1, source_target_pairs={{0,16},{8,24},{16,0},{24,8},{1,17},{9,25},{17,1},{25,9},{2,18},{10... | collective-permute-start | bytes 245768 | tf_op jit(solution)/shard_map/ppermute | solution.py:466
  130.4 8.7 %collective-permute-start.38 = (bf16[64,640]{1,0:T(8,128)(2,1)S(1)}, bf16[64,640]{1,0:T(8,128)(2,1)S(1)}, u32[]{:S(2)}, u32[]{:S(2)}) collective-permute-start(bf16[64,640]{1,0:T(8,128)(2,1)S(1)} %get-tuple-element.233), channel_id=1, source_target_pairs={{0,24},{8,0},{16,8},{24,16},{1,25},{9,1},{17,9},{25,17},{2,26},{10... | collective-permute-start | bytes 245768 | tf_op jit(solution)/shard_map/ppermute | solution.py:466
  (23 other events, 125.3 us)
